TPU v7x, 32 devices: a whole 2x2x4 slice. The times are simulated.
32 devices in a mesh: batch: 8 (over z, x), tensor: 4 (over y, core).
Axes of the slice: x: 2, y: 2, z: 4, core: 2. Of those that a mesh axis runs over, the one named last changes fastest.
Arguments:
- tokens: bfloat16 [2, 8192, 768], P(None, 'batch'), may hold values from -6 to 6
- lengths: int32 [2, 8, 1024], P(None, 'batch'), may hold values from 0 to 512, as said below
- quarters: int32 [2], replicated, may hold values from 1 to 4, as said below
- query_weight: bfloat16 [768, 768], P(None, 'tensor'), may hold values from -0.3125 to 0.3125
- query_bias: float32 [768], P('tensor'), may hold values from -4 to 4
- key_weight: bfloat16 [768, 768], P(None, 'tensor'), may hold values from -0.3125 to 0.3125
- value_weight: bfloat16 [768, 768], P(None, 'tensor'), may hold values from -0.21875 to 0.21875
- value_bias: float32 [768], P('tensor'), may hold values from -6 to 6
- out_weight: bfloat16 [768, 768], P('tensor'), may hold values from -0.625 to 0.625
- out_bias: float32 [768], replicated, may hold values from -6 to 6
- norm1_gain: float32 [768], replicated, may hold values from 0.5 to 1.5
- norm1_shift: float32 [768], replicated, may hold values from -4 to 4
- in_weight: bfloat16 [768, 3072], P(None, 'tensor'), may hold values from -0.21875 to 0.21875
- in_bias: float32 [3072], P('tensor'), may hold values from -6 to 6
- down_weight: bfloat16 [3072, 768], P('tensor'), may hold values from -0.109375 to 0.109375
- down_bias: float32 [768], replicated, may hold values from -6 to 6
- norm2_gain: float32 [768], replicated, may hold values from 0.5 to 1.5
- norm2_shift: float32 [768], replicated, may hold values from -4 to 4
- cotangent: bfloat16 [2, 8192, 768], P(None, 'batch'), may hold values from -6 to 6
Outputs:
- layer_out: bfloat16 [2, 8192, 768], P(None, ('batch', 'tensor'))
- input_grad: float32 [2, 8192, 768], P(None, ('batch', 'tensor'))
- query_weight_grad: float32 [768, 768], P(None, 'tensor')
- query_bias_grad: float32 [768], P('tensor')
- key_weight_grad: float32 [768, 768], P(None, 'tensor')
- value_weight_grad: float32 [768, 768], P(None, 'tensor')
- value_bias_grad: float32 [768], P('tensor')
- out_weight_grad: float32 [768, 768], P('tensor')
- out_bias_grad: float32 [768], replicated
- norm1_gain_grad: float32 [768], replicated
- norm1_shift_grad: float32 [768], replicated
- in_weight_grad: float32 [768, 3072], P(None, 'tensor')
- in_bias_grad: float32 [3072], P('tensor')
- down_weight_grad: float32 [3072, 768], P('tensor')
- down_bias_grad: float32 [768], replicated
- norm2_gain_grad: float32 [768], replicated
- norm2_shift_grad: float32 [768], replicated
Inputs may be any that keep to these rules, and one draw needn't show every extreme that they name: Row lengths[m, b] lists, in order, the lengths of the sequences packed into block b of micro-batch m; they sum to 1024, and 0 marks an unused slot. In every micro-batch one block holds a sequence of exactly 512 tokens. Micro-batch m keeps the first 12 * quarters[m] / 4 heads and the first 3072 * quarters[m] / 4 units; exactly one micro-batch has quarters 4.
All inputs are finite; a program needn't handle non-finite values.
Results may differ from a plain program's by a relative error of at most 0.013.
The roundings to bfloat16 on the way count: a program that leaves them out, or rounds other values in their place, can miss the bound.
Values may be sent and summed in bfloat16 or wider, within the bound.
A program may use at most 128 MiB of HBM per device.

v0:
```python
import functools

import jax
import jax.numpy as jnp
from jax import lax
from jax.experimental import pallas as pl
from jax.experimental.pallas import tpu as pltpu
from jax.sharding import PartitionSpec as P

HEADS = 12
HEAD_DIM = 64
FF = 3072
EPSILON = 1e-12
ROOT_HALF = 0.7071067811865476
DENSITY_SCALE = 0.3989422804014327
QB = 256
WIDE = 256

BF = jnp.bfloat16
F32 = jnp.float32
MESH = pl.DeviceIdType.MESH


def layer_norm(values_in, gain, shift):
    row_mean = jnp.mean(values_in, axis=-1, keepdims=True)
    centred = values_in - row_mean
    inverse = lax.rsqrt(jnp.mean(centred * centred, axis=-1, keepdims=True) + EPSILON)
    normed = centred * inverse
    return (normed * gain + shift, normed, inverse)


def norm_back(grad_in, normed, inverse, gain):
    spread = grad_in * gain
    return inverse * (
        spread
        - jnp.mean(spread, axis=-1, keepdims=True)
        - normed * jnp.mean(spread * normed, axis=-1, keepdims=True)
    )


def cross_dot(left, right):
    return lax.dot_general(left, right, (((0,), (0,)), ((), ())), preferred_element_type=F32)


def back_dot(left, right):
    return lax.dot_general(left, right, (((1,), (1,)), ((), ())), preferred_element_type=F32)


def lane_half(tile, which):
    lane = lax.broadcasted_iota(jnp.int32, tile.shape, 1)
    return jnp.where((lane >= HEAD_DIM) == (which == 1), tile, jnp.zeros_like(tile))


def tile_lanes(kind, tile):
    start = 128 * kind + 384 * tile
    return slice(start, start + 128)


def column_of(row):
    return jnp.transpose(jnp.broadcast_to(row, (8, row.shape[1])))[:, 0:1]


def attend_kernel(
    place, live, tokens, lengths, query_weight, key_weight, value_weight, query_bias,
    value_bias, out_weight,
    qkv, log_total, context, partial, segment, weight,
    value_t, bias, seg_col,
):
    micro, step = pl.program_id(0), pl.program_id(1)
    rows_all = tokens.shape[1]

    @pl.when((micro == 0) & (step == 0))
    def _():
        bias[...] = jnp.zeros_like(bias)
        for kind, ref in enumerate((query_weight, key_weight, value_weight)):
            weight[:, 128 * kind : 128 * kind + 128] = ref[:, 0:128]
            weight[:, 384 + 128 * kind : 448 + 128 * kind] = ref[:, 128:192]
            weight[:, 448 + 128 * kind : 512 + 128 * kind] = jnp.zeros_like(ref[:, 128:192])
        for kind, ref in ((0, query_bias), (2, value_bias)):
            bias[0:1, 128 * kind : 128 * kind + 128] = ref[0:1, 0:128]
            bias[0:1, 384 + 128 * kind : 448 + 128 * kind] = ref[0:1, 128:192]

    @pl.when(step == 0)
    def _():
        def project(index, carry):
            rows = pl.ds(pl.multiple_of(index * QB, QB), QB)
            qkv[rows, :] = (
                jnp.dot(tokens[0, rows, :], weight[...], preferred_element_type=F32)
                + bias[0:1, :]
            ).astype(BF)
            for tile in range(2):
                value_t[128 * tile : 128 * tile + 128, rows] = jnp.transpose(
                    qkv[rows, tile_lanes(2, tile)]
                )
            return carry

        lax.fori_loop(0, rows_all // QB, project, 0)
        ends = jnp.broadcast_to(lengths[0], (8, rows_all))
        lane = lax.broadcasted_iota(jnp.int32, (8, rows_all), 1)
        shift = 1
        while shift < rows_all:
            ends = ends + jnp.where(lane >= shift, pltpu.roll(ends, shift, 1), 0)
            shift *= 2
        ends_col = column_of(ends[0:1, :].astype(F32))
        places = lax.broadcasted_iota(jnp.int32, (rows_all, rows_all), 1).astype(F32)
        count = jnp.sum(jnp.where(ends_col <= places, 1.0, 0.0), axis=0, keepdims=True)
        segment[...] = jnp.broadcast_to(count, (8, rows_all))
        seg_col[...] = column_of(count)

    rows = pl.ds(pl.multiple_of(step * QB, QB), QB)
    same = seg_col[...] == segment[0:1, rows]
    outs = []
    logs = []
    for head in range(3):
        tile = head // 2
        query = qkv[rows, tile_lanes(0, tile)] * jnp.asarray(0.125, BF)
        query = lane_half(query, head % 2)
        keys = qkv[:, tile_lanes(1, tile)]
        scores = jnp.where(same, back_dot(keys, query), -1e30)
        top = jnp.max(scores, axis=0, keepdims=True)
        expo = jnp.exp(scores - top)
        total = jnp.sum(expo, axis=0, keepdims=True)
        probs = (expo * (1.0 / total)).astype(BF)
        outs.append(
            jnp.dot(
                value_t[64 * head : 64 * head + 64, :], probs, preferred_element_type=F32
            )
        )
        logs.append(top + jnp.log(total))
    context_t = jnp.concatenate(outs, axis=0) * live[micro].astype(F32)
    low = jnp.transpose(context_t).astype(BF)
    context[...] = low
    log_total[...] = jnp.concatenate(logs + [jnp.zeros((5, QB), F32)], axis=0)
    partial[...] = jnp.dot(low, out_weight[...], preferred_element_type=F32).astype(BF)


def attend(
    place, live, tokens, lengths, query_weight, key_weight, value_weight, query_bias,
    value_bias, out_weight,
):
    micro_count, rows, width = tokens.shape
    steps = rows // QB
    full = lambda array: pl.BlockSpec(array.shape, lambda m, i, *_: (0,) * array.ndim)
    return pl.pallas_call(
        attend_kernel,
        grid_spec=pltpu.PrefetchScalarGridSpec(
            num_scalar_prefetch=2,
            grid=(micro_count, steps),
            in_specs=[
                pl.BlockSpec((1, rows, width), lambda m, i, *_: (m, 0, 0)),
                pl.BlockSpec((1, 1, rows), lambda m, i, *_: (m, 0, 0)),
                full(query_weight),
                full(key_weight),
                full(value_weight),
                full(query_bias),
                full(value_bias),
                full(out_weight),
            ],
            out_specs=[
                pl.BlockSpec((rows, 3 * WIDE), lambda m, i, *_: (m, 0)),
                pl.BlockSpec((8, QB), lambda m, i, *_: (m, i)),
                pl.BlockSpec((QB, 192), lambda m, i, *_: (m * steps + i, 0)),
                pl.BlockSpec((QB, width), lambda m, i, p, l: (m * steps + (i ^ p[0]), 0)),
                pl.BlockSpec((8, rows), lambda m, i, *_: (m, 0)),
                pl.BlockSpec((width, 3 * WIDE), lambda m, i, *_: (0, 0)),
            ],
            scratch_shapes=[
                pltpu.VMEM((WIDE, rows), BF),
                pltpu.VMEM((8, 3 * WIDE), F32),
                pltpu.VMEM((rows, 1), F32),
            ],
        ),
        out_shape=[
            jax.ShapeDtypeStruct((micro_count * rows, 3 * WIDE), BF),
            jax.ShapeDtypeStruct((micro_count * 8, rows), F32),
            jax.ShapeDtypeStruct((micro_count * rows, 192), BF),
            jax.ShapeDtypeStruct((micro_count * rows, width), BF),
            jax.ShapeDtypeStruct((micro_count * 8, rows), F32),
            jax.ShapeDtypeStruct((width, 3 * WIDE), BF),
        ],
        compiler_params=pltpu.CompilerParams(
            dimension_semantics=("arbitrary", "arbitrary"), vmem_limit_bytes=48 << 20
        ),
        name="attend",
    )(
        place, live, tokens, lengths, query_weight, key_weight, value_weight, query_bias,
        value_bias, out_weight,
    )


CHUNK = 48


def by_chunks(count, body):
    def one(index, carry):
        body(pl.multiple_of(index * CHUNK, CHUNK))
        return carry

    lax.fori_loop(0, count // CHUNK, one, 0)


def reduce_plan(rows, order):
    plan = []
    length, offset = rows, 0
    for bit in order:
        halving = length % (2 * CHUNK) == 0
        if halving:
            length //= 2
        plan.append((bit, halving, length, offset))
        offset += length
    return plan, offset


class BatchSum:
    def __init__(self, term, first, rows, columns, order, give, take, whole, sems, base):
        self.term, self.first, self.rows, self.columns = term, first, rows, columns
        self.give, self.take, self.whole = give, take, whole
        self.send_sem, self.recv_sem = sems
        self.base = base
        self.plan, _ = reduce_plan(rows, order)
        self.place = lax.axis_index("batch")
        self.starts = [0]
        for bit, halving, length, _ in self.plan:
            start = self.starts[-1]
            if halving:
                start = start + ((self.place >> bit) & 1) * length
            self.starts.append(start)

    def rows_at(self, ref, start, length, lift=0):
        return ref.at[pl.ds(pl.multiple_of(start + lift, CHUNK), length), 0 : self.columns]

    def copy(self, src, dst, index, bit):
        return pltpu.make_async_remote_copy(
            src_ref=src,
            dst_ref=dst,
            send_sem=self.send_sem.at[self.base + index],
            recv_sem=self.recv_sem.at[self.base + index],
            device_id={"batch": self.place ^ (1 << bit)},
            device_id_type=MESH,
        )

    def reduce_copy(self, step):
        bit, _, length, offset = self.plan[step]
        return self.copy(
            self.rows_at(self.give, offset, length),
            self.rows_at(self.take, offset, length),
            step,
            bit,
        )

    def reduce_start(self, step):
        bit, halving, length, offset = self.plan[step]
        start = self.starts[step]
        if halving:
            start = start + (1 - ((self.place >> bit) & 1)) * length

        def pack(at):
            self.rows_at(self.give, offset + at, CHUNK)[...] = self.rows_at(
                self.term, start + at, CHUNK, self.first
            )[...].astype(BF)

        by_chunks(length, pack)
        self.reduce_copy(step).start()

    def reduce_finish(self, step):
        _, halving, length, offset = self.plan[step]
        self.reduce_copy(step).wait_recv()
        start = self.starts[step + 1]

        def merge(at):
            mine = self.rows_at(self.term, start + at, CHUNK, self.first)
            got = self.rows_at(self.take, offset + at, CHUNK)[...].astype(F32)
            if halving:
                mine[...] = mine[...] + got
            else:
                mine[...] = self.rows_at(self.give, offset + at, CHUNK)[...].astype(F32) + got

        by_chunks(length, merge)

    def settle(self):
        length, start = self.plan[-1][2], self.starts[-1]

        def pack(at):
            self.rows_at(self.whole, start + at, CHUNK)[...] = self.rows_at(
                self.term, start + at, CHUNK, self.first
            )[...].astype(BF)

        by_chunks(length, pack)

    def gather_copy(self, step):
        bit, _, length, _ = self.plan[step]
        region = self.rows_at(self.whole, self.starts[step + 1], length)
        return self.copy(region, region, len(self.plan) + step, bit)

    def gather_start(self, step):
        if self.plan[step][1]:
            self.gather_copy(step).start()

    def gather_finish(self, step):
        if self.plan[step][1]:
            self.gather_copy(step).wait_recv()

    def advance(self, index):
        count = len(self.plan)
        if index == 0:
            self.reduce_start(0)
        elif index < count:
            self.reduce_finish(index - 1)
            self.reduce_start(index)
        elif index == count:
            self.reduce_finish(count - 1)
            self.settle()
            self.gather_start(count - 1)
        elif index < 2 * count:
            self.gather_finish(2 * count - index)
            self.gather_start(2 * count - index - 1)
        else:
            self.gather_finish(0)

            def widen(at):
                self.rows_at(self.term, at, CHUNK, self.first)[...] = self.rows_at(
                    self.whole, at, CHUNK
                )[...].astype(F32)

            by_chunks(self.rows, widen)

    def drain(self):
        for step in range(len(self.plan)):
            self.reduce_copy(step).wait_send()
            if self.plan[step][1]:
                self.gather_copy(step).wait_send()


class VectorSum:
    def __init__(self, values, take, targets, sems, base):
        self.values, self.take, self.targets = values, take, targets
        self.send_sem, self.recv_sem = sems
        self.base = base

    def at(self, ref, step):
        return ref.at[8 * step : 8 * step + 8, :]

    def copy(self, step):
        return pltpu.make_async_remote_copy(
            src_ref=self.at(self.values, step),
            dst_ref=self.at(self.take, step),
            send_sem=self.send_sem.at[self.base + step],
            recv_sem=self.recv_sem.at[self.base + step],
            device_id=self.targets[step],
            device_id_type=MESH,
        )

    def advance(self, index):
        if index > 0:
            self.copy(index - 1).wait_recv()
            self.at(self.values, index)[...] = (
                self.at(self.values, index - 1)[...] + self.at(self.take, index - 1)[...]
            )
        if index < len(self.targets):
            self.copy(index).start()

    def drain(self):
        for step in range(len(self.targets)):
            self.copy(step).wait_send()


def layer_kernel(
    live, partials, token_hbm, cot_hbm, qkv_hbm, in_weight, down_weight, weight_all, out_weight,
    context, log_total, segment, vectors,
    result, input_grad, in_term, down_term, qkv_term, out_term, sums_out, bias_out,
    far, near, cross, sums, hid, gm2, act, slope, gpre, pbuf, grad_low,
    hidden_rows, normed_rows, inverse_rows, key_t, key_acc, value_acc, seg_col, out_wide,
    down_take, down_whole, in_take, in_whole, low_take, low_whole, high_take, high_whole,
    out_take, out_whole, vec_values, vec_take, bias_values, bias_take,
    send_sem, recv_sem, batch_send, batch_recv, load_sem,
):
    place = lax.axis_index("tensor")
    batch_place = lax.axis_index("batch")
    batch_bits = lax.axis_size("batch").bit_length() - 1
    core_id = {"tensor": place ^ 1}
    chip_id = {"tensor": place ^ 2}
    share = input_grad.shape[1]
    rows_all = 4 * share

    def slot(buf, micro, index):
        start = (micro * 4 + index) * share
        if not isinstance(start, int):
            start = pl.multiple_of(start, share)
        return buf.at[pl.ds(start, share), :]

    def own_rows(buf, micro):
        start = micro * share
        if not isinstance(start, int):
            start = pl.multiple_of(start, share)
        return buf.at[pl.ds(start, share), :]

    def copy(src, dst, micro, phase, kind, target):
        index = (micro * 4 + phase) * 6 + kind
        return pltpu.make_async_remote_copy(
            src_ref=src,
            dst_ref=dst,
            send_sem=send_sem.at[index],
            recv_sem=recv_sem.at[index],
            device_id=target,
            device_id_type=MESH,
        )

    def far_copy(parts, micro, phase):
        return copy(slot(parts, micro, 3), own_rows(far, micro), micro, phase, 0, core_id)

    def near_copy(parts, micro, phase):
        return copy(slot(parts, micro, 1), own_rows(near, micro), micro, phase, 1, core_id)

    def cross_copy(micro, phase):
        return copy(own_rows(sums, micro), own_rows(cross, micro), micro, phase, 2, chip_id)

    def crossing_copy(buf, micro, phase):
        return copy(slot(buf, micro, 0), slot(buf, micro, 2), micro, phase, 3, chip_id)

    def beside_copy(buf, micro, phase):
        return copy(slot(buf, micro, 0), slot(buf, micro, 1), micro, phase, 4, core_id)

    def onward_copy(buf, micro, phase):
        return copy(slot(buf, micro, 2), slot(buf, micro, 3), micro, phase, 5, core_id)

    def scatter_start(parts, micro, phase):
        far_copy(parts, micro, phase).start()
        near_copy(parts, micro, phase).start()

    def scatter_mid(parts, micro, phase):
        far_copy(parts, micro, phase).wait_recv()
        own_rows(sums, micro)[...] = (
            slot(parts, micro, 2)[...].astype(F32) + own_rows(far, micro)[...].astype(F32)
        ).astype(BF)
        cross_copy(micro, phase).start()

    def scatter_end(parts, micro, phase):
        near_copy(parts, micro, phase).wait_recv()
        cross_copy(micro, phase).wait_recv()
        cross_copy(micro, phase).wait_send()
        return (
            slot(parts, micro, 0)[...].astype(F32)
            + own_rows(near, micro)[...].astype(F32)
            + own_rows(cross, micro)[...].astype(F32)
        )

    def scatter_drain(parts, micro, phase):
        far_copy(parts, micro, phase).wait_send()
        near_copy(parts, micro, phase).wait_send()

    def gather_start(buf, micro, phase):
        crossing_copy(buf, micro, phase).start()
        beside_copy(buf, micro, phase).start()

    def gather_step(buf, micro, phase, which):
        @pl.when(which == 1)
        def _():
            beside_copy(buf, micro, phase).wait_recv()

        @pl.when(which == 2)
        def _():
            crossing_copy(buf, micro, phase).wait_recv()
            onward_copy(buf, micro, phase).start()

        @pl.when(which == 3)
        def _():
            onward_copy(buf, micro, phase).wait_recv()

    def gather_drain(buf, micro, phase):
        crossing_copy(buf, micro, phase).wait_send()
        beside_copy(buf, micro, phase).wait_send()
        onward_copy(buf, micro, phase).wait_send()

    def vector(index):
        return vectors[index : index + 1, :]

    def tally(index, value):
        vec_values[index : index + 1, :] += jnp.sum(value, axis=0, keepdims=True)

    def load_rows(hbm, target, micro, index):
        start = pl.multiple_of(place * share, share)
        return pltpu.make_async_copy(
            hbm.at[micro, pl.ds(start, share), :], target, load_sem.at[index]
        )

    token_loads = [load_rows(token_hbm, slot(grad_low, m, 0), m, m) for m in range(2)]
    cot_loads = [load_rows(cot_hbm, result.at[m], m, 2 + m) for m in range(2)]
    for load in token_loads + cot_loads:
        load.start()

    sems = (batch_send, batch_recv)
    up = tuple(range(batch_bits))
    turned = up[1:] + up[:1]
    stride = 2 * batch_bits

    def carve(buf, sizes):
        start = 0
        views = []
        for size in sizes:
            views.append(buf.at[start : start + size, :])
            start += size
        return views

    down_give, in_give, out_give = carve(
        slope, (down_take.shape[0], in_take.shape[0], out_take.shape[0])
    )
    low_give, high_give = carve(hid, (low_take.shape[0], high_take.shape[0]))
    down_sum = BatchSum(
        down_term, 0, 768, 768, up, down_give, down_take, down_whole, sems, 0
    )
    in_sum = BatchSum(in_term, 0, 768, 768, turned, in_give, in_take, in_whole, sems, stride)
    low_sum = BatchSum(
        qkv_term, 0, 384, 640, up, low_give, low_take, low_whole, sems, 2 * stride
    )
    high_sum = BatchSum(
        qkv_term, 384, 384, 640, turned, high_give, high_take, high_whole, sems, 3 * stride
    )
    out_sum = BatchSum(
        out_term, 0, 192, 768, turned, out_give, out_take, out_whole, sems, 4 * stride
    )
    batch_targets = [{"batch": batch_place ^ (1 << bit)} for bit in up]
    shared_sum = VectorSum(
        vec_values, vec_take, batch_targets + [core_id, chip_id], sems, 5 * stride
    )
    bias_sum = VectorSum(bias_values, bias_take, batch_targets, sems, 6 * stride + 2)

    barrier = pltpu.get_barrier_semaphore()
    partners = [core_id, chip_id] + batch_targets
    for target in partners:
        pl.semaphore_signal(barrier, inc=1, device_id=target, device_id_type=MESH)
    vec_values[0:8, :] = jnp.zeros((8, vec_values.shape[1]), F32)
    bias_values[0:8, :] = jnp.zeros((8, bias_values.shape[1]), F32)
    out_term[...] = jnp.zeros_like(out_term)
    out_wide[0:192, :] = out_weight[...]
    out_wide[192:256, :] = jnp.zeros((64, out_wide.shape[1]), BF)
    pl.semaphore_wait(barrier, len(partners))

    for micro in range(2):
        scatter_start(partials, micro, 0)
    for micro in range(2):
        scatter_mid(partials, micro, 0)
    for load in token_loads + cot_loads:
        load.wait()

    def opening(micro, carry):
        total = scatter_end(partials, micro, 0)
        hidden, normed, inverse = layer_norm(
            slot(grad_low, micro, 0)[...].astype(F32) + total + vector(0), vector(1), vector(2)
        )
        own_rows(hidden_rows, micro)[...] = hidden
        own_rows(normed_rows, micro)[...] = normed
        own_rows(inverse_rows, micro)[...] = jnp.broadcast_to(inverse, (share, 128))
        slot(hid, micro, 0)[...] = hidden.astype(BF)
        gather_start(hid, micro, 0)
        return carry

    lax.fori_loop(0, 2, opening, 0)

    def forward(index, carry):
        micro, which = index // 4, index % 4
        gather_step(hid, micro, 0, which)
        pre = (
            jnp.dot(slot(hid, micro, which)[...], in_weight[...], preferred_element_type=F32)
            + vector(3)
        )
        alive = live[micro].astype(F32)
        below = 0.5 * (1.0 + lax.erf(pre * ROOT_HALF)) * alive
        low = (pre * below).astype(BF)
        slot(act, micro, which)[...] = low
        slot(slope, micro, which)[...] = (
            below + pre * jnp.exp(-0.5 * pre * pre) * (DENSITY_SCALE * alive)
        ).astype(BF)
        slot(pbuf, micro, which)[...] = jnp.dot(
            low, down_weight[...], preferred_element_type=F32
        ).astype(BF)

        @pl.when(which == 3)
        def _():
            scatter_start(pbuf, micro, 1)

        @pl.when(index == 4)
        def _():
            scatter_mid(pbuf, 0, 1)

        return carry

    lax.fori_loop(0, 8, forward, 0)
    scatter_mid(pbuf, 1, 1)

    def middle(micro, carry):
        total = scatter_end(pbuf, micro, 1)
        final, normed, inverse = layer_norm(
            own_rows(hidden_rows, micro)[...] + total + vector(4), vector(5), vector(6)
        )
        grad_y = result[micro].astype(F32)
        result[micro] = final.astype(BF)
        grad_mid2 = norm_back(grad_y, normed, inverse, vector(5))
        own_rows(hidden_rows, micro)[...] = grad_mid2
        slot(gm2, micro, 0)[...] = grad_mid2.astype(BF)
        gather_start(gm2, micro, 1)
        tally(3, grad_mid2)
        tally(4, grad_y * normed)
        tally(5, grad_y)
        return carry

    lax.fori_loop(0, 2, middle, 0)
    for micro in range(2):
        scatter_drain(pbuf, micro, 1)

    def backward(index, carry):
        micro, which = index // 4, index % 4
        gather_step(gm2, micro, 1, which)
        grad_pre = (
            back_dot(slot(gm2, micro, which)[...], down_weight[...])
            * slot(slope, micro, which)[...].astype(F32)
        ).astype(BF)
        slot(gpre, micro, which)[...] = grad_pre
        tally(6, grad_pre.astype(F32))
        slot(pbuf, micro, which)[...] = back_dot(grad_pre, in_weight[...]).astype(BF)

        @pl.when(which == 3)
        def _():
            scatter_start(pbuf, micro, 2)

        @pl.when(index == 4)
        def _():
            scatter_mid(pbuf, 0, 2)

        return carry

    lax.fori_loop(0, 8, backward, 0)
    scatter_mid(pbuf, 1, 2)

    def weigh(left, right, out):
        def block(index, carry):
            lanes = pl.ds(pl.multiple_of(index * 256, 256), 256)
            out[lanes, :] = cross_dot(left[:, lanes], right[...])
            return carry

        lax.fori_loop(0, out.shape[0] // 256, block, 0)

    weigh(act, gm2, down_term)
    down_sum.advance(0)
    for micro in range(2):
        gather_drain(hid, micro, 0)
        gather_drain(gm2, micro, 1)
    token_all = [
        pltpu.make_async_copy(
            token_hbm.at[m], act.at[pl.ds(m * rows_all, rows_all), :], load_sem.at[4 + m]
        )
        for m in range(2)
    ]
    qkv_all = pltpu.make_async_copy(qkv_hbm, gm2, load_sem.at[6])
    for load in token_all:
        load.start()
    qkv_all.start()
    weigh(hid, gpre, in_term)
    in_sum.advance(0)

    def closing(micro, carry):
        total = scatter_end(pbuf, micro, 2)
        grad_hidden = own_rows(hidden_rows, micro)[...] + total
        normed = own_rows(normed_rows, micro)[...]
        inverse = own_rows(inverse_rows, micro)[:, 0:1]
        grad = norm_back(grad_hidden, normed, inverse, vector(1))
        input_grad[micro] = grad
        slot(grad_low, micro, 0)[...] = grad.astype(BF)
        gather_start(grad_low, micro, 2)
        tally(0, grad)
        tally(1, grad_hidden * normed)
        tally(2, grad_hidden)
        return carry

    lax.fori_loop(0, 2, closing, 0)
    for micro in range(2):
        scatter_drain(pbuf, micro, 2)
    shared_sum.advance(0)
    for load in token_all:
        load.wait()
    qkv_all.wait()
    qkv, tokens, grads = gm2, act, gpre

    def micro_rows(micro):
        return pl.ds(pl.multiple_of(micro * rows_all, rows_all), rows_all)

    def finish_micro(micro):
        block = micro_rows(micro)
        for tile in range(2):
            lanes = slice(128 * tile, 128 * tile + 128)
            grads[block, tile_lanes(1, tile)] = key_acc[:, lanes].astype(BF)
            grads[block, tile_lanes(2, tile)] = value_acc[:, lanes].astype(BF)
        bias_values[0:1, :] += jnp.sum(grads[block, :].astype(F32), axis=0, keepdims=True)

        def send_slot(index, carry):
            start = pl.multiple_of(micro * rows_all + (index ^ place) * share, share)
            slot(pbuf, micro, index)[...] = back_dot(
                grads[pl.ds(start, share), :], weight_all[...]
            ).astype(BF)
            return carry

        lax.fori_loop(0, 4, send_slot, 0)
        scatter_start(pbuf, micro, 3)

    def attend_back(index, carry):
        micro, which = index // 4, index % 4
        gather_step(grad_low, micro, 2, which)
        step = which ^ place
        block = micro_rows(micro)
        rows = pl.ds(pl.multiple_of(micro * rows_all + step * share, share), share)

        @pl.when(which == 0)
        def _():
            for tile in range(2):
                key_t[128 * tile : 128 * tile + 128, :] = jnp.transpose(
                    qkv[block, tile_lanes(1, tile)]
                )
            key_acc[...] = jnp.zeros_like(key_acc)
            value_acc[...] = jnp.zeros_like(value_acc)
            seg_col[...] = column_of(
                segment[pl.ds(pl.multiple_of(micro * 8, 8), 8), :][0:1, :]
            )

        eight = pl.ds(pl.multiple_of(micro * 8, 8), 8)
        columns = pl.ds(pl.multiple_of(step * share, share), share)
        seg_row = segment[eight, columns][0:1, :]
        logs = log_total[eight, columns]
        grad_slot = slot(grad_low, micro, which)[...]
        out_term[...] += cross_dot(context[rows, :], grad_slot)

        @pl.when(index == 7)
        def _():
            out_sum.advance(0)

        alive = live[micro].astype(BF)
        grad_context = back_dot(grad_slot, out_wide[...]).astype(BF) * alive
        same = seg_col[...] == seg_row
        query_parts = []
        for head in range(3):
            tile = head // 2
            lanes = slice(128 * tile, 128 * tile + 128)
            query = qkv[rows, tile_lanes(0, tile)] * jnp.asarray(0.125, BF)
            query = lane_half(query, head % 2)
            grad_tile = lane_half(grad_context[:, lanes], head % 2)
            keys = qkv[block, tile_lanes(1, tile)]
            values = qkv[block, tile_lanes(2, tile)]
            scores = jnp.where(same, back_dot(keys, query), -1e30)
            probs = jnp.exp(scores - logs[head : head + 1, :])
            grad_probs = back_dot(values, grad_tile)
            mean = jnp.sum(probs * grad_probs, axis=0, keepdims=True)
            grad_scores = (probs * (grad_probs - mean)).astype(BF)
            value_acc[:, lanes] += jnp.dot(
                probs.astype(BF), grad_tile, preferred_element_type=F32
            )
            key_acc[:, lanes] += jnp.dot(grad_scores, query, preferred_element_type=F32)
            query_parts.append(
                jnp.dot(
                    key_t[64 * head : 64 * head + 64, :],
                    grad_scores,
                    preferred_element_type=F32,
                )
            )
        query_t = jnp.concatenate(query_parts + [jnp.zeros((64, share), F32)], axis=0) * 0.125
        query_grad = jnp.transpose(query_t).astype(BF)
        for tile in range(2):
            grads[rows, tile_lanes(0, tile)] = query_grad[:, 128 * tile : 128 * tile + 128]

        @pl.when(which == 3)
        def _():
            finish_micro(micro)

        def at(point, *events):
            @pl.when(index == point)
            def _():
                for event in events:
                    event()

        at(0, lambda: shared_sum.advance(1))
        at(1, lambda: down_sum.advance(1), lambda: in_sum.advance(1))
        at(2, lambda: shared_sum.advance(2))
        at(3, lambda: down_sum.advance(2), lambda: in_sum.advance(2))
        at(4, lambda: scatter_mid(pbuf, 0, 3), lambda: down_sum.advance(3))
        at(5, lambda: in_sum.advance(3), lambda: down_sum.advance(4))
        at(6, lambda: in_sum.advance(4), lambda: shared_sum.advance(3))
        return carry

    lax.fori_loop(0, 8, attend_back, 0)

    def weigh_qkv(index, carry):
        lanes = pl.ds(pl.multiple_of(index * 256, 256), 256)
        qkv_term[lanes, :] = cross_dot(tokens[:, lanes], grads[...])
        qkv_term[lanes, 448:512] = qkv_term[lanes, 512:576]
        qkv_term[lanes, 512:640] = qkv_term[lanes, 640:768]
        return carry

    lax.fori_loop(0, 3, weigh_qkv, 0)
    low_sum.advance(0)
    high_sum.advance(0)
    bias_sum.advance(0)
    scatter_mid(pbuf, 1, 3)

    def final_rows(micro):
        input_grad[micro] = input_grad[micro] + scatter_end(pbuf, micro, 3)

    last = 2 * batch_bits
    final_rows(0)
    out_sum.advance(1)
    queue = []
    for step in range(1, last + 1):
        queue.append((low_sum, step))
        queue.append((high_sum, step))
        if step < last:
            queue.append((out_sum, step + 1))
        if 4 + step <= last:
            queue.append((down_sum, 4 + step))
            queue.append((in_sum, 4 + step))
        if 1 <= step <= batch_bits:
            queue.append((bias_sum, step))
        if 3 + step <= batch_bits + 2:
            queue.append((shared_sum, 3 + step))
        if step == 3:
            queue.append((None, step))
    for owner, step in queue:
        if owner is None:
            final_rows(1)
        else:
            owner.advance(step)

    base = 8 * batch_bits
    sums_out[...] = vec_values[base + 16 : base + 24, :]
    sums_out[6:7, :] = vec_values[base + 6 : base + 7, :]
    bias_out[...] = bias_values[base : base + 8, :]
    for micro in range(2):
        scatter_drain(partials, micro, 0)
        scatter_drain(pbuf, micro, 3)
        gather_drain(grad_low, micro, 2)
    for owner in (down_sum, in_sum, low_sum, high_sum, out_sum, shared_sum, bias_sum):
        owner.drain()


def layer_call(
    live, partials, tokens, cotangent, qkv, in_weight, down_weight, weight_all, out_weight,
    context, log_total, segment, vectors,
):
    micro_count, rows_all, width = tokens.shape
    share = rows_all // 4
    rows = micro_count * rows_all
    units = in_weight.shape[1]
    batch_bits = lax.axis_size("batch").bit_length() - 1
    order = tuple(range(batch_bits))
    vmem = pl.BlockSpec(memory_space=pltpu.VMEM)
    hbm = pl.BlockSpec(memory_space=pl.ANY)
    smem = pl.BlockSpec(memory_space=pltpu.SMEM)

    def exchange(count, columns):
        total = reduce_plan(count, order)[1]
        return [pltpu.VMEM((total, columns), BF), pltpu.VMEM((count, columns), BF)]

    batch_sems = 7 * 2 * batch_bits + 2
    return pl.pallas_call(
        layer_kernel,
        in_specs=[smem, vmem, hbm, hbm, hbm] + [vmem] * 8,
        out_specs=[vmem] * 8,
        out_shape=[
            jax.ShapeDtypeStruct((micro_count, share, width), BF),
            jax.ShapeDtypeStruct((micro_count, share, width), F32),
            jax.ShapeDtypeStruct((width, units), F32),
            jax.ShapeDtypeStruct((units, width), F32),
            jax.ShapeDtypeStruct((width, 3 * WIDE), F32),
            jax.ShapeDtypeStruct((192, width), F32),
            jax.ShapeDtypeStruct((8, width), F32),
            jax.ShapeDtypeStruct((8, width), F32),
        ],
        scratch_shapes=[
            pltpu.VMEM((2 * share, width), BF),
            pltpu.VMEM((2 * share, width), BF),
            pltpu.VMEM((2 * share, width), BF),
            pltpu.VMEM((2 * share, width), BF),
            pltpu.VMEM((rows, width), BF),
            pltpu.VMEM((rows, width), BF),
            pltpu.VMEM((rows, units), BF),
            pltpu.VMEM((rows, units), BF),
            pltpu.VMEM((rows, units), BF),
            pltpu.VMEM((rows, width), BF),
            pltpu.VMEM((rows, width), BF),
            pltpu.VMEM((2 * share, width), F32),
            pltpu.VMEM((2 * share, width), F32),
            pltpu.VMEM((2 * share, 128), F32),
            pltpu.VMEM((WIDE, rows_all), BF),
            pltpu.VMEM((rows_all, WIDE), F32),
            pltpu.VMEM((rows_all, WIDE), F32),
            pltpu.VMEM((rows_all, 1), F32),
            pltpu.VMEM((WIDE, width), BF),
        ]
        + exchange(768, 768)
        + exchange(768, 768)
        + exchange(384, 640)
        + exchange(384, 640)
        + exchange(192, 768)
        + [
            pltpu.VMEM((8 * (batch_bits + 3), width), F32),
            pltpu.VMEM((8 * (batch_bits + 2), width), F32),
            pltpu.VMEM((8 * (batch_bits + 1), width), F32),
            pltpu.VMEM((8 * batch_bits, width), F32),
            pltpu.SemaphoreType.DMA((48,)),
            pltpu.SemaphoreType.DMA((48,)),
            pltpu.SemaphoreType.DMA((batch_sems,)),
            pltpu.SemaphoreType.DMA((batch_sems,)),
            pltpu.SemaphoreType.DMA((7,)),
        ],
        compiler_params=pltpu.CompilerParams(
            collective_id=1, has_side_effects=True, vmem_limit_bytes=67_043_328
        ),
        name="layer",
    )(
        live, partials, tokens, cotangent, qkv, in_weight, down_weight, weight_all, out_weight,
        context, log_total, segment, vectors,
    )


def local(
    tokens,
    lengths,
    quarters,
    query_weight,
    query_bias,
    key_weight,
    value_weight,
    value_bias,
    out_weight,
    out_bias,
    norm1_gain,
    norm1_shift,
    in_weight,
    in_bias,
    down_weight,
    down_bias,
    norm2_gain,
    norm2_shift,
    cotangent,
):
    place = lax.axis_index("tensor").astype(jnp.int32)
    live = (4 * place < 4 * quarters).astype(jnp.int32)
    qkv, log_total, context, partials, segment, weight_all = attend(
        place[None],
        live,
        tokens,
        lengths.reshape(lengths.shape[0], 1, lengths.shape[2]),
        query_weight,
        key_weight,
        value_weight,
        query_bias[None],
        value_bias[None],
        out_weight,
    )
    vectors = jnp.stack(
        [out_bias, norm1_gain, norm1_shift, in_bias, down_bias, norm2_gain, norm2_shift, out_bias]
    )
    result, input_grad, in_sum, down_sum, packed, out_sum, sums, bias = layer_call(
        live,
        partials,
        tokens,
        cotangent,
        qkv,
        in_weight,
        down_weight,
        weight_all,
        out_weight,
        context,
        log_total,
        segment,
        vectors,
    )
    query_sum = jnp.concatenate([packed[:, 0:128], packed[:, 384:448]], axis=1)
    key_sum = jnp.concatenate([packed[:, 128:256], packed[:, 448:512]], axis=1)
    value_sum = jnp.concatenate([packed[:, 256:384], packed[:, 512:576]], axis=1)
    query_bias_sum = jnp.concatenate([bias[0, 0:128], bias[0, 384:448]])
    value_bias_sum = jnp.concatenate([bias[0, 256:384], bias[0, 640:704]])
    return (
        result,
        input_grad,
        query_sum,
        query_bias_sum,
        key_sum,
        value_sum,
        value_bias_sum,
        out_sum,
        sums[0],
        sums[1],
        sums[2],
        in_sum,
        sums[6],
        down_sum,
        sums[3],
        sums[4],
        sums[5],
    )


def solution(mesh):
    in_specs = (
        P(None, "batch", None),
        P(None, "batch", None),
        P(),
        P(None, "tensor"),
        P("tensor"),
        P(None, "tensor"),
        P(None, "tensor"),
        P("tensor"),
        P("tensor", None),
        P(),
        P(),
        P(),
        P(None, "tensor"),
        P("tensor"),
        P("tensor", None),
        P(),
        P(),
        P(),
        P(None, "batch", None),
    )
    out_specs = (
        P(None, ("batch", "tensor"), None),
        P(None, ("batch", "tensor"), None),
        P(None, "tensor"),
        P("tensor"),
        P(None, "tensor"),
        P(None, "tensor"),
        P("tensor"),
        P("tensor", None),
        P(),
        P(),
        P(),
        P(None, "tensor"),
        P("tensor"),
        P("tensor", None),
        P(),
        P(),
        P(),
    )
    return jax.shard_map(local, mesh=mesh, in_specs=in_specs, out_specs=out_specs, check_vma=False)
```

profile of v0, /device:TPU:0, one launch (start us, length us, event | category | flops | bytes accessed | tf_op | source)
XLA Modules:
  0.0 271.5 jit_solution(1476001667072257461)
XLA Ops:
  0.7 0.0 copy-start.1
  0.7 0.7 compare_convert_fusion.live
  1.4 0.0 copy-start.6
  1.4 0.7 stack.25
  2.1 0.7 stack.26
  2.8 0.7 stack.27
  3.4 0.7 stack.28
  4.1 0.7 stack.29
  4.8 0.7 stack.30
  5.5 0.7 stack.31
  6.2 0.6 stack.32.vectors
  6.9 1.1 copy.36.query_weight
  8.0 1.1 copy.37.key_weight
  9.1 1.1 copy.38.value_weight
  10.3 0.0 copy-done.1
  10.3 0.0 copy-start.5
  10.3 0.7 copy-done.5
  11.0 0.0 copy-start.7
  11.0 0.7 copy-done.7
  11.7 0.0 copy-start.8
  11.7 0.7 copy-done.8
  12.3 34.7 %attend.1 = (bf16[2048,768]{1,0:T(8,128)(2,1)}, f32[16,1024]{1,0:T(8,128)S(1)}, bf16[2048,192]{1,0:T(8,128)(2,1)S(1)}, bf16[2048,768]{1,0:T(8,128)(2,1)}, f32[16...) custom-call(s32[1]{0:T(128)} %bitcast.place, s32[2]{0:T(128)S(1)} %compare_convert_fusion.live, ...), custom_call_target="tpu_custom_call" | custom-call | tf_op jit(solution)/shard_map/attend/pallas_call | solution.py:144
  47.0 0.0 copy-done.6
  47.0 0.0 copy-start
  47.0 1.0 copy-done
  48.0 0.0 copy-start.2
  48.0 1.0 copy-done.2
  49.0 0.0 copy-start.3
  49.0 0.6 copy-done.3
  49.6 0.0 copy-start.4
  49.6 0.6 copy-done.4
  50.3 203.9 %layer.1 = (bf16[2,256,768]{2,1,0:T(8,128)(2,1)}, f32[2,256,768]{2,1,0:T(8,128)}, f32[768,768]{1,0:T(8,128)}, f32[768,768]{1,0:T(8,128)}, f32[768,768]{1,0:T(8,1...) custom-call(s32[2]{0:T(128)} %copy-done.6, bf16[2048,768]{1,0:T(8,128)(2,1)} %get-tuple-element.31.partials, ...), custom_call_target="tpu_custom_call" | custom-call | tf_op jit(solution)/shard_map/layer/pallas_call | solution.py:859
  254.1 0.0 copy-start.11
  254.2 0.8 slice_bitcast_fusion.1
  255.0 0.7 slice_bitcast_fusion
  255.7 0.6 pad_maximum_fusion.3
  256.3 1.8 slice_reduce_fusion
  258.1 1.5 fusion.1
  259.6 0.0 copy-done.11
  259.6 0.1 fusion
  259.6 0.1 pad_maximum_fusion.2
  259.7 1.1 copy.41
  260.8 0.1 pad_maximum_fusion
  260.9 0.0 copy-start.12
  260.9 1.1 copy.39
  262.0 1.1 copy.40
  263.0 0.0 copy-start.13
  263.0 2.1 copy.47
  265.2 0.0 copy-done.12
  265.2 0.0 copy-start.10
  265.2 1.1 copy.48
  266.3 0.0 copy-done.13
  266.3 0.8 copy.49
  267.1 0.5 copy-done.10
  267.6 0.0 copy-start.9
  267.6 1.4 copy.50
  269.0 1.1 copy-done.9
  270.1 1.4 copy.51
Async XLA Ops:
  0.7 9.6 %copy-start.1 = (bf16[192,768]{1,0:T(8,128)(2,1)S(1)}, bf16[192,768]{1,0:T(8,128)(2,1)}, u32[]{:S(2)}) copy-start(bf16[192,768]{1,0:T(8,128)(2,1)} %out_weight.3) | copy-start | bytes 884740
  1.4 45.6 %copy-start.6 = (s32[2]{0:T(128)}, s32[2]{0:T(128)S(1)}, u32[]{:S(2)}) copy-start(s32[2]{0:T(128)S(1)} %compare_convert_fusion.live) | copy-start | bytes 28
  10.3 0.7 copy-start.5
  11.0 0.7 copy-start.7
  11.7 0.7 copy-start.8
  47.0 1.0 copy-start
  48.0 1.0 copy-start.2
  49.0 0.6 copy-start.3
  49.6 0.6 copy-start.4
  254.1 5.4 %copy-start.11 = (f32[768,768]{1,0:T(8,128)S(1)}, f32[768,768]{1,0:T(8,128)}, u32[]{:S(2)}) copy-start(f32[768,768]{1,0:T(8,128)} %get-tuple-element.39) | copy-start | bytes 7077892
  260.9 4.3 %copy-start.12 = (f32[2,256,768]{2,1,0:T(8,128)S(1)}, f32[2,256,768]{2,1,0:T(8,128)}, u32[]{:S(2)}) copy-start(f32[2,256,768]{2,1,0:T(8,128)} %get-tuple-element.101) | copy-start | bytes 4718596
  263.0 3.3 %copy-start.13 = (f32[192,768]{1,0:T(8,128)S(1)}, f32[192,768]{1,0:T(8,128)}, u32[]{:S(2)}) copy-start(f32[192,768]{1,0:T(8,128)} %get-tuple-element.107) | copy-start | bytes 1769476
  265.2 2.4 copy-start.10
  267.6 2.5 copy-start.9
where the time goes:
time: 272 us
  Pallas kernels  239 us (88%)
  local copies, waits for them, and re-layouts  30.8 us (11%)
    pallas_call x1, Pallas kernels, layer_call(): pl.pallas_call(layer_kernel, in_specs=[smem, vmem, hbm, hbm, hbm] + [vmem...  204 us
    pallas_call x1, Pallas kernels, attend(): pl.pallas_call(attend_kernel, grid_spec=pltpu.PrefetchScalarGridSpec(num_...  34.7 us
    unnamed x39, local copies, waits for them, and re-layouts  20.4 us
    another operation x8, local copies, waits for them, and re-layouts, local(): jnp.stack([out_bias, norm1_gain, norm1_shift, in_bias, down_bias, norm2_g...  5.47 us

commit v1 on v0

--- a/solution.py
+++ b/solution.py
@@ -63,8 +63,8 @@
 def attend_kernel(
     place, live, tokens, lengths, query_weight, key_weight, value_weight, query_bias,
     value_bias, out_weight,
-    qkv, log_total, context, partial, segment, weight,
-    value_t, bias, seg_col,
+    qkv, log_total, context, partial, segment,
+    weight, value_t, bias, seg_col,
 ):
     micro, step = pl.program_id(0), pl.program_id(1)
     rows_all = tokens.shape[1]
@@ -73,9 +73,9 @@
     def _():
         bias[...] = jnp.zeros_like(bias)
         for kind, ref in enumerate((query_weight, key_weight, value_weight)):
-            weight[:, 128 * kind : 128 * kind + 128] = ref[:, 0:128]
-            weight[:, 384 + 128 * kind : 448 + 128 * kind] = ref[:, 128:192]
-            weight[:, 448 + 128 * kind : 512 + 128 * kind] = jnp.zeros_like(ref[:, 128:192])
+            weight[128 * kind : 128 * kind + 128, :] = ref[0:128, :]
+            weight[384 + 128 * kind : 448 + 128 * kind, :] = ref[128:192, :]
+            weight[448 + 128 * kind : 512 + 128 * kind, :] = jnp.zeros_like(ref[128:192, :])
         for kind, ref in ((0, query_bias), (2, value_bias)):
             bias[0:1, 128 * kind : 128 * kind + 128] = ref[0:1, 0:128]
             bias[0:1, 384 + 128 * kind : 448 + 128 * kind] = ref[0:1, 128:192]
@@ -85,8 +85,7 @@
         def project(index, carry):
             rows = pl.ds(pl.multiple_of(index * QB, QB), QB)
             qkv[rows, :] = (
-                jnp.dot(tokens[0, rows, :], weight[...], preferred_element_type=F32)
-                + bias[0:1, :]
+                back_dot(tokens[0, rows, :], weight[...]) + bias[0:1, :]
             ).astype(BF)
             for tile in range(2):
                 value_t[128 * tile : 128 * tile + 128, rows] = jnp.transpose(
@@ -162,9 +161,9 @@
                 pl.BlockSpec((QB, 192), lambda m, i, *_: (m * steps + i, 0)),
                 pl.BlockSpec((QB, width), lambda m, i, p, l: (m * steps + (i ^ p[0]), 0)),
                 pl.BlockSpec((8, rows), lambda m, i, *_: (m, 0)),
-                pl.BlockSpec((width, 3 * WIDE), lambda m, i, *_: (0, 0)),
             ],
             scratch_shapes=[
+                pltpu.VMEM((3 * WIDE, width), BF),
                 pltpu.VMEM((WIDE, rows), BF),
                 pltpu.VMEM((8, 3 * WIDE), F32),
                 pltpu.VMEM((rows, 1), F32),
@@ -176,7 +175,6 @@
             jax.ShapeDtypeStruct((micro_count * rows, 192), BF),
             jax.ShapeDtypeStruct((micro_count * rows, width), BF),
             jax.ShapeDtypeStruct((micro_count * 8, rows), F32),
-            jax.ShapeDtypeStruct((width, 3 * WIDE), BF),
         ],
         compiler_params=pltpu.CompilerParams(
             dimension_semantics=("arbitrary", "arbitrary"), vmem_limit_bytes=48 << 20
@@ -202,8 +200,8 @@
 def reduce_plan(rows, order):
     plan = []
     length, offset = rows, 0
-    for bit in order:
-        halving = length % (2 * CHUNK) == 0
+    for index, bit in enumerate(order):
+        halving = index < len(order) - 1 and length % (2 * CHUNK) == 0
         if halving:
             length //= 2
         plan.append((bit, halving, length, offset))
@@ -281,7 +279,7 @@
         length, start = self.plan[-1][2], self.starts[-1]
 
         def pack(at):
-            self.rows_at(self.whole, start + at, CHUNK)[...] = self.rows_at(
+            self.rows_at(self.whole, start + at, CHUNK, self.first)[...] = self.rows_at(
                 self.term, start + at, CHUNK, self.first
             )[...].astype(BF)
 
@@ -289,7 +287,7 @@
 
     def gather_copy(self, step):
         bit, _, length, _ = self.plan[step]
-        region = self.rows_at(self.whole, self.starts[step + 1], length)
+        region = self.rows_at(self.whole, self.starts[step + 1], length, self.first)
         return self.copy(region, region, len(self.plan) + step, bit)
 
     def gather_start(self, step):
@@ -299,6 +297,9 @@
     def gather_finish(self, step):
         if self.plan[step][1]:
             self.gather_copy(step).wait_recv()
+
+    def last(self):
+        return 2 * len(self.plan) - 1
 
     def advance(self, index):
         count = len(self.plan)
@@ -310,19 +311,11 @@
         elif index == count:
             self.reduce_finish(count - 1)
             self.settle()
-            self.gather_start(count - 1)
-        elif index < 2 * count:
-            self.gather_finish(2 * count - index)
-            self.gather_start(2 * count - index - 1)
+            self.gather_start(count - 2)
         else:
-            self.gather_finish(0)
-
-            def widen(at):
-                self.rows_at(self.term, at, CHUNK, self.first)[...] = self.rows_at(
-                    self.whole, at, CHUNK
-                )[...].astype(F32)
-
-            by_chunks(self.rows, widen)
+            self.gather_finish(2 * count - 1 - index)
+            if index < 2 * count - 1:
+                self.gather_start(2 * count - 2 - index)
 
     def drain(self):
         for step in range(len(self.plan)):
@@ -364,14 +357,90 @@
             self.copy(step).wait_send()
 
 
+EVENTS = {
+    "open": (
+        "d0", "d2",
+    ),
+    "closing": (
+        "d1", "d3",
+    ),
+    "closed": (
+        "s",
+    ),
+    0: (
+        "d0", "d2", "i0", "d1",
+    ),
+    1: (
+        "s", "d3", "i1",
+    ),
+    2: (
+        "i0", "i2", "d2", "i3",
+    ),
+    3: (
+        "s", "i1", "d3", "d0", "d1", "i2",
+    ),
+    "between": (
+        "i0", "d2", "i3",
+    ),
+    "weighed": (
+        "i1",
+    ),
+    4: (
+        "d3", "d2", "d0",
+    ),
+    5: (
+        "s", "d1",
+    ),
+    6: (
+        "s", "d3", "i0", "i2",
+    ),
+    7: (
+        "s", "i1", "i3", "d0",
+    ),
+    "start": (
+        "i0", "d1",
+    ),
+    "pre": (
+        "i1", "i2",
+    ),
+    "mid": (
+        "q0",
+    ),
+    "tail": (
+        "o0", "i3", "q1", "q0", "o0", "q2", "q1", "q0",
+    ),
+    "end": (
+        "i2", "q2", "q1", "i3", "q0", "o0", "q2", "q1", "q0", "o0",
+        "q2", "q1", "o0", "q2",
+    ),
+}
+Z_FIRST = ("d0", "d1", "o0",)
+POINTS = (
+    "open", "closing", "closed", 0, 1, 2, 3, "between", "weighed", 4, 5, 6, 7,
+    "start", "pre", "mid", "tail", "end",
+)
+
+
 def layer_kernel(
-    live, partials, token_hbm, cot_hbm, qkv_hbm, in_weight, down_weight, weight_all, out_weight,
-    context, log_total, segment, vectors,
-    result, input_grad, in_term, down_term, qkv_term, out_term, sums_out, bias_out,
+    live, partial_hbm, token_hbm, cot_hbm, qkv_hbm, in_hbm, down_hbm, query_hbm, key_hbm,
+    value_hbm, out_hbm, context_hbm, log_total, segment, *rest
+):
+    layer_body(
+        live, partial_hbm, token_hbm, cot_hbm, qkv_hbm, in_hbm, down_hbm,
+        (query_hbm, key_hbm, value_hbm), out_hbm, context_hbm, log_total, segment,
+        rest[:7], *rest[7:]
+    )
+
+
+def layer_body(
+    live, partial_hbm, token_hbm, cot_hbm, qkv_hbm, in_hbm, down_hbm, low_hbm, out_hbm,
+    context_hbm, log_total, segment, vectors,
+    result, input_grad, in_whole, down_whole, qkv_whole, out_whole, sums_out, bias_out,
+    in_weight, down_weight, context,
+    in_term, down_term, qkv_term, out_term, weight_all,
     far, near, cross, sums, hid, gm2, act, slope, gpre, pbuf, grad_low,
     hidden_rows, normed_rows, inverse_rows, key_t, key_acc, value_acc, seg_col, out_wide,
-    down_take, down_whole, in_take, in_whole, low_take, low_whole, high_take, high_whole,
-    out_take, out_whole, vec_values, vec_take, bias_values, bias_take,
+    down_take, in_take, qkv_take, out_take, vec_values, vec_take, bias_values, bias_take,
     send_sem, recv_sem, batch_send, batch_recv, load_sem,
 ):
     place = lax.axis_index("tensor")
@@ -472,57 +541,79 @@
         onward_copy(buf, micro, phase).wait_send()
 
     def vector(index):
-        return vectors[index : index + 1, :]
+        return vectors[index][...].reshape(1, -1)
 
     def tally(index, value):
         vec_values[index : index + 1, :] += jnp.sum(value, axis=0, keepdims=True)
 
-    def load_rows(hbm, target, micro, index):
-        start = pl.multiple_of(place * share, share)
-        return pltpu.make_async_copy(
-            hbm.at[micro, pl.ds(start, share), :], target, load_sem.at[index]
-        )
-
-    token_loads = [load_rows(token_hbm, slot(grad_low, m, 0), m, m) for m in range(2)]
-    cot_loads = [load_rows(cot_hbm, result.at[m], m, 2 + m) for m in range(2)]
-    for load in token_loads + cot_loads:
-        load.start()
+    taken = []
+
+    def load(src, dst):
+        taken.append(0)
+        handle = pltpu.make_async_copy(src, dst, load_sem.at[len(taken) - 1])
+        handle.start()
+        return handle
+
+    def micro_block(micro):
+        return pl.ds(micro * rows_all, rows_all)
+
+    first_row = pl.multiple_of(place * share, share)
+    part_loads = [
+        load(partial_hbm.at[micro_block(m), :], pbuf.at[micro_block(m), :]) for m in range(2)
+    ]
+    row_loads = [
+        load(token_hbm.at[m, pl.ds(first_row, share), :], slot(grad_low, m, 0))
+        for m in range(2)
+    ] + [load(cot_hbm.at[m, pl.ds(first_row, share), :], result.at[m]) for m in range(2)]
+    weight_loads = [load(in_hbm, in_weight), load(down_hbm, down_weight)]
+    late_loads = [load(out_hbm, out_wide.at[0:192, :]), load(context_hbm, context)]
+    for kind, ref in enumerate(low_hbm):
+        late_loads.append(
+            load(ref.at[0:128, :], weight_all.at[128 * kind : 128 * kind + 128, :])
+        )
+        late_loads.append(
+            load(ref.at[128:192, :], weight_all.at[384 + 64 * kind : 448 + 64 * kind, :])
+        )
 
     sems = (batch_send, batch_recv)
     up = tuple(range(batch_bits))
     turned = up[1:] + up[:1]
     stride = 2 * batch_bits
-
-    def carve(buf, sizes):
-        start = 0
-        views = []
-        for size in sizes:
-            views.append(buf.at[start : start + size, :])
-            start += size
-        return views
-
-    down_give, in_give, out_give = carve(
-        slope, (down_take.shape[0], in_take.shape[0], out_take.shape[0])
-    )
-    low_give, high_give = carve(hid, (low_take.shape[0], high_take.shape[0]))
-    down_sum = BatchSum(
-        down_term, 0, 768, 768, up, down_give, down_take, down_whole, sems, 0
-    )
-    in_sum = BatchSum(in_term, 0, 768, 768, turned, in_give, in_take, in_whole, sems, stride)
-    low_sum = BatchSum(
-        qkv_term, 0, 384, 640, up, low_give, low_take, low_whole, sems, 2 * stride
-    )
-    high_sum = BatchSum(
-        qkv_term, 384, 384, 640, turned, high_give, high_take, high_whole, sems, 3 * stride
-    )
-    out_sum = BatchSum(
-        out_term, 0, 192, 768, turned, out_give, out_take, out_whole, sems, 4 * stride
-    )
+    chunks = []
+
+    def chunk(term, first, count, order, give, give_at, take, take_at, whole):
+        size = reduce_plan(count, order)[1]
+        chunks.append(
+            BatchSum(
+                term, first, count, term.shape[1], order,
+                give.at[give_at : give_at + size, :],
+                take.at[take_at : take_at + size, :],
+                whole, sems, len(chunks) * stride,
+            )
+        )
+        return chunks[-1]
+
+    small = reduce_plan(192, up)[1]
+    named = {}
+
+    def add_chunks(letter, count, term, give, give_at, take, whole):
+        for k in range(count):
+            name = letter + str(k)
+            named[name] = chunk(
+                term, 192 * k, 192, turned if name in Z_FIRST else up,
+                *((slope, small * (4 + k)) if letter == "i" and k < 2 else (give, give_at + small * k)),
+                take, small * k, whole,
+            )
+
+    add_chunks("d", 4, down_term, slope, 0, down_take, down_whole)
+    add_chunks("i", 4, in_term, hid, small * 2, in_take, in_whole)
+    add_chunks("q", 3, qkv_term, hid, 0, qkv_take, qkv_whole)
+    add_chunks("o", 1, out_term, hid, small * 3, out_take, out_whole)
     batch_targets = [{"batch": batch_place ^ (1 << bit)} for bit in up]
     shared_sum = VectorSum(
-        vec_values, vec_take, batch_targets + [core_id, chip_id], sems, 5 * stride
+        vec_values, vec_take, batch_targets + [core_id, chip_id], sems, 12 * stride
     )
-    bias_sum = VectorSum(bias_values, bias_take, batch_targets, sems, 6 * stride + 2)
+    bias_sum = VectorSum(bias_values, bias_take, batch_targets, sems, 13 * stride + 2)
 
     barrier = pltpu.get_barrier_semaphore()
     partners = [core_id, chip_id] + batch_targets
@@ -531,19 +622,20 @@
     vec_values[0:8, :] = jnp.zeros((8, vec_values.shape[1]), F32)
     bias_values[0:8, :] = jnp.zeros((8, bias_values.shape[1]), F32)
     out_term[...] = jnp.zeros_like(out_term)
-    out_wide[0:192, :] = out_weight[...]
     out_wide[192:256, :] = jnp.zeros((64, out_wide.shape[1]), BF)
+    weight_all[576:640, :] = jnp.zeros((64, weight_all.shape[1]), BF)
     pl.semaphore_wait(barrier, len(partners))
 
     for micro in range(2):
-        scatter_start(partials, micro, 0)
+        part_loads[micro].wait()
+        scatter_start(pbuf, micro, 0)
     for micro in range(2):
-        scatter_mid(partials, micro, 0)
-    for load in token_loads + cot_loads:
-        load.wait()
+        scatter_mid(pbuf, micro, 0)
+    for handle in row_loads + weight_loads:
+        handle.wait()
 
     def opening(micro, carry):
-        total = scatter_end(partials, micro, 0)
+        total = scatter_end(pbuf, micro, 0)
         hidden, normed, inverse = layer_norm(
             slot(grad_low, micro, 0)[...].astype(F32) + total + vector(0), vector(1), vector(2)
         )
@@ -555,6 +647,8 @@
         return carry
 
     lax.fori_loop(0, 2, opening, 0)
+    for micro in range(2):
+        scatter_drain(pbuf, micro, 0)
 
     def forward(index, carry):
         micro, which = index // 4, index % 4
@@ -640,24 +734,20 @@
         lax.fori_loop(0, out.shape[0] // 256, block, 0)
 
     weigh(act, gm2, down_term)
-    down_sum.advance(0)
+    for k in range(4):
+        named["d" + str(k)].advance(0)
     for micro in range(2):
         gather_drain(hid, micro, 0)
         gather_drain(gm2, micro, 1)
-    token_all = [
-        pltpu.make_async_copy(
-            token_hbm.at[m], act.at[pl.ds(m * rows_all, rows_all), :], load_sem.at[4 + m]
-        )
-        for m in range(2)
-    ]
-    qkv_all = pltpu.make_async_copy(qkv_hbm, gm2, load_sem.at[6])
-    for load in token_all:
-        load.start()
-    qkv_all.start()
+    late_loads.extend(
+        load(token_hbm.at[m], act.at[micro_block(m), :]) for m in range(2)
+    )
+    late_loads.append(load(qkv_hbm, gm2))
     weigh(hid, gpre, in_term)
-    in_sum.advance(0)
-
-    def closing(micro, carry):
+    for k in range(4):
+        named["i" + str(k)].advance(0)
+
+    def closing(micro):
         total = scatter_end(pbuf, micro, 2)
         grad_hidden = own_rows(hidden_rows, micro)[...] + total
         normed = own_rows(normed_rows, micro)[...]
@@ -669,32 +759,59 @@
         tally(0, grad)
         tally(1, grad_hidden * normed)
         tally(2, grad_hidden)
-        return carry
-
-    lax.fori_loop(0, 2, closing, 0)
+
+    reached = {name: 0 for name in named}
+    reached["s"] = -1
+    planned = {}
+    for point in POINTS:
+        planned[point] = []
+        for name in EVENTS.get(point, ()):
+            reached[name] += 1
+            planned[point].append((name, reached[name]))
+
+    def run(point):
+        for name, step in planned[point]:
+            (shared_sum if name == "s" else named[name]).advance(step)
+
+    run("open")
+    closing(0)
+    run("closing")
+    closing(1)
     for micro in range(2):
         scatter_drain(pbuf, micro, 2)
-    shared_sum.advance(0)
-    for load in token_all:
-        load.wait()
-    qkv_all.wait()
+    run("closed")
+    for handle in late_loads:
+        handle.wait()
     qkv, tokens, grads = gm2, act, gpre
 
     def micro_rows(micro):
         return pl.ds(pl.multiple_of(micro * rows_all, rows_all), rows_all)
 
-    def finish_micro(micro):
-        block = micro_rows(micro)
-        for tile in range(2):
-            lanes = slice(128 * tile, 128 * tile + 128)
-            grads[block, tile_lanes(1, tile)] = key_acc[:, lanes].astype(BF)
-            grads[block, tile_lanes(2, tile)] = value_acc[:, lanes].astype(BF)
-        bias_values[0:1, :] += jnp.sum(grads[block, :].astype(F32), axis=0, keepdims=True)
-
+    def finish_grads(micro):
+        block = micro_block(micro)
+        grads[block, 128:256] = key_acc[:, 0:128].astype(BF)
+        grads[block, 256:384] = value_acc[:, 0:128].astype(BF)
+        grads[block, 448:512] = key_acc[:, 128:192].astype(BF)
+        grads[block, 512:640] = value_acc[:, 128:256].astype(BF)
+        bias_values[0:1, 0:640] += jnp.sum(
+            grads[block, 0:640].astype(F32), axis=0, keepdims=True
+        )
+
+
+    def weigh_low(micro):
+        block = micro_block(micro)
+        for first, count in ((0, 256), (256, 256), (512, 64)):
+            value = cross_dot(grads[block, first : first + count], tokens[block, :])
+            if micro == 0:
+                qkv_term[first : first + count, :] = value
+            else:
+                qkv_term[first : first + count, :] += value
+
+    def send_input(micro):
         def send_slot(index, carry):
             start = pl.multiple_of(micro * rows_all + (index ^ place) * share, share)
-            slot(pbuf, micro, index)[...] = back_dot(
-                grads[pl.ds(start, share), :], weight_all[...]
+            slot(pbuf, micro, index)[...] = jnp.dot(
+                grads[pl.ds(start, share), 0:640], weight_all[...], preferred_element_type=F32
             ).astype(BF)
             return carry
 
@@ -729,7 +846,7 @@
 
         @pl.when(index == 7)
         def _():
-            out_sum.advance(0)
+            named["o0"].advance(0)
 
         alive = live[micro].astype(BF)
         grad_context = back_dot(grad_slot, out_wide[...]).astype(BF) * alive
@@ -761,85 +878,73 @@
             )
         query_t = jnp.concatenate(query_parts + [jnp.zeros((64, share), F32)], axis=0) * 0.125
         query_grad = jnp.transpose(query_t).astype(BF)
-        for tile in range(2):
-            grads[rows, tile_lanes(0, tile)] = query_grad[:, 128 * tile : 128 * tile + 128]
-
-        @pl.when(which == 3)
+        grads[rows, 0:128] = query_grad[:, 0:128]
+        grads[rows, 384:448] = query_grad[:, 128:192]
+
+        for point in range(8):
+            if planned[point]:
+
+                @pl.when(index == point)
+                def _():
+                    run(point)
+
+        @pl.when(index == 3)
         def _():
-            finish_micro(micro)
-
-        def at(point, *events):
-            @pl.when(index == point)
-            def _():
-                for event in events:
-                    event()
-
-        at(0, lambda: shared_sum.advance(1))
-        at(1, lambda: down_sum.advance(1), lambda: in_sum.advance(1))
-        at(2, lambda: shared_sum.advance(2))
-        at(3, lambda: down_sum.advance(2), lambda: in_sum.advance(2))
-        at(4, lambda: scatter_mid(pbuf, 0, 3), lambda: down_sum.advance(3))
-        at(5, lambda: in_sum.advance(3), lambda: down_sum.advance(4))
-        at(6, lambda: in_sum.advance(4), lambda: shared_sum.advance(3))
+            finish_grads(0)
+            send_input(0)
+            run("between")
+            weigh_low(0)
+            run("weighed")
+
+        @pl.when(index == 4)
+        def _():
+            scatter_mid(pbuf, 0, 3)
+
         return carry
 
     lax.fori_loop(0, 8, attend_back, 0)
-
-    def weigh_qkv(index, carry):
-        lanes = pl.ds(pl.multiple_of(index * 256, 256), 256)
-        qkv_term[lanes, :] = cross_dot(tokens[:, lanes], grads[...])
-        qkv_term[lanes, 448:512] = qkv_term[lanes, 512:576]
-        qkv_term[lanes, 512:640] = qkv_term[lanes, 640:768]
-        return carry
-
-    lax.fori_loop(0, 3, weigh_qkv, 0)
-    low_sum.advance(0)
-    high_sum.advance(0)
+    finish_grads(1)
+    weigh_low(1)
+    for k in range(3):
+        named["q" + str(k)].advance(0)
     bias_sum.advance(0)
+    run("start")
+    send_input(1)
+    run("pre")
     scatter_mid(pbuf, 1, 3)
+    run("mid")
 
     def final_rows(micro):
         input_grad[micro] = input_grad[micro] + scatter_end(pbuf, micro, 3)
 
-    last = 2 * batch_bits
     final_rows(0)
-    out_sum.advance(1)
-    queue = []
-    for step in range(1, last + 1):
-        queue.append((low_sum, step))
-        queue.append((high_sum, step))
-        if step < last:
-            queue.append((out_sum, step + 1))
-        if 4 + step <= last:
-            queue.append((down_sum, 4 + step))
-            queue.append((in_sum, 4 + step))
-        if 1 <= step <= batch_bits:
-            queue.append((bias_sum, step))
-        if 3 + step <= batch_bits + 2:
-            queue.append((shared_sum, 3 + step))
-        if step == 3:
-            queue.append((None, step))
-    for owner, step in queue:
-        if owner is None:
-            final_rows(1)
-        else:
-            owner.advance(step)
+    run("tail")
+    final_rows(1)
+    for index in range(1, batch_bits + 1):
+        bias_sum.advance(index)
+    run("end")
+    for name in sorted(named):
+        while reached[name] < named[name].last():
+            reached[name] += 1
+            named[name].advance(reached[name])
+    while reached["s"] < batch_bits + 2:
+        reached["s"] += 1
+        shared_sum.advance(reached["s"])
 
     base = 8 * batch_bits
     sums_out[...] = vec_values[base + 16 : base + 24, :]
     sums_out[6:7, :] = vec_values[base + 6 : base + 7, :]
     bias_out[...] = bias_values[base : base + 8, :]
     for micro in range(2):
-        scatter_drain(partials, micro, 0)
         scatter_drain(pbuf, micro, 3)
         gather_drain(grad_low, micro, 2)
-    for owner in (down_sum, in_sum, low_sum, high_sum, out_sum, shared_sum, bias_sum):
+    for owner in chunks + [shared_sum, bias_sum]:
         owner.drain()
 
 
 def layer_call(
-    live, partials, tokens, cotangent, qkv, in_weight, down_weight, weight_all, out_weight,
-    context, log_total, segment, vectors,
+    live, partials, tokens, cotangent, qkv, in_weight, down_weight, query_weight, key_weight,
+    value_weight, out_weight, context, log_total, segment, *vectors
 ):
     micro_count, rows_all, width = tokens.shape
     share = rows_all // 4
@@ -847,30 +952,34 @@
     units = in_weight.shape[1]
     batch_bits = lax.axis_size("batch").bit_length() - 1
     order = tuple(range(batch_bits))
+    small = reduce_plan(192, order)[1]
     vmem = pl.BlockSpec(memory_space=pltpu.VMEM)
     hbm = pl.BlockSpec(memory_space=pl.ANY)
     smem = pl.BlockSpec(memory_space=pltpu.SMEM)
-
-    def exchange(count, columns):
-        total = reduce_plan(count, order)[1]
-        return [pltpu.VMEM((total, columns), BF), pltpu.VMEM((count, columns), BF)]
-
-    batch_sems = 7 * 2 * batch_bits + 2
+    batch_sems = 14 * 2 * batch_bits + 2
     return pl.pallas_call(
         layer_kernel,
-        in_specs=[smem, vmem, hbm, hbm, hbm] + [vmem] * 8,
+        in_specs=[smem] + [hbm] * 11 + [vmem] * (2 + len(vectors)),
         out_specs=[vmem] * 8,
         out_shape=[
             jax.ShapeDtypeStruct((micro_count, share, width), BF),
             jax.ShapeDtypeStruct((micro_count, share, width), F32),
-            jax.ShapeDtypeStruct((width, units), F32),
-            jax.ShapeDtypeStruct((units, width), F32),
-            jax.ShapeDtypeStruct((width, 3 * WIDE), F32),
-            jax.ShapeDtypeStruct((192, width), F32),
+            jax.ShapeDtypeStruct((width, units), BF),
+            jax.ShapeDtypeStruct((units, width), BF),
+            jax.ShapeDtypeStruct((576, width), BF),
+            jax.ShapeDtypeStruct((192, width), BF),
             jax.ShapeDtypeStruct((8, width), F32),
             jax.ShapeDtypeStruct((8, width), F32),
         ],
         scratch_shapes=[
+            pltpu.VMEM((width, units), BF),
+            pltpu.VMEM((units, width), BF),
+            pltpu.VMEM((rows, 192), BF),
+            pltpu.VMEM((width, units), F32),
+            pltpu.VMEM((units, width), F32),
+            pltpu.VMEM((576, width), F32),
+            pltpu.VMEM((192, width), F32),
+            pltpu.VMEM((640, width), BF),
             pltpu.VMEM((2 * share, width), BF),
             pltpu.VMEM((2 * share, width), BF),
             pltpu.VMEM((2 * share, width), BF),
@@ -890,13 +999,10 @@
             pltpu.VMEM((rows_all, WIDE), F32),
             pltpu.VMEM((rows_all, 1), F32),
             pltpu.VMEM((WIDE, width), BF),
-        ]
-        + exchange(768, 768)
-        + exchange(768, 768)
-        + exchange(384, 640)
-        + exchange(384, 640)
-        + exchange(192, 768)
-        + [
+            pltpu.VMEM((4 * small, width), BF),
+            pltpu.VMEM((4 * small, width), BF),
+            pltpu.VMEM((3 * small, width), BF),
+            pltpu.VMEM((small, width), BF),
             pltpu.VMEM((8 * (batch_bits + 3), width), F32),
             pltpu.VMEM((8 * (batch_bits + 2), width), F32),
             pltpu.VMEM((8 * (batch_bits + 1), width), F32),
@@ -905,15 +1011,15 @@
             pltpu.SemaphoreType.DMA((48,)),
             pltpu.SemaphoreType.DMA((batch_sems,)),
             pltpu.SemaphoreType.DMA((batch_sems,)),
-            pltpu.SemaphoreType.DMA((7,)),
+            pltpu.SemaphoreType.DMA((20,)),
         ],
         compiler_params=pltpu.CompilerParams(
             collective_id=1, has_side_effects=True, vmem_limit_bytes=67_043_328
         ),
         name="layer",
     )(
-        live, partials, tokens, cotangent, qkv, in_weight, down_weight, weight_all, out_weight,
-        context, log_total, segment, vectors,
+        live, partials, tokens, cotangent, qkv, in_weight, down_weight, query_weight,
+        key_weight, value_weight, out_weight, context, log_total, segment, *vectors
     )
 
 
@@ -940,20 +1046,16 @@
 ):
     place = lax.axis_index("tensor").astype(jnp.int32)
     live = (4 * place < 4 * quarters).astype(jnp.int32)
-    qkv, log_total, context, partials, segment, weight_all = attend(
+    low_weights = (query_weight.T, key_weight.T, value_weight.T)
+    qkv, log_total, context, partials, segment = attend(
         place[None],
         live,
         tokens,
         lengths.reshape(lengths.shape[0], 1, lengths.shape[2]),
-        query_weight,
-        key_weight,
-        value_weight,
+        *low_weights,
         query_bias[None],
         value_bias[None],
         out_weight,
-    )
-    vectors = jnp.stack(
-        [out_bias, norm1_gain, norm1_shift, in_bias, down_bias, norm2_gain, norm2_shift, out_bias]
     )
     result, input_grad, in_sum, down_sum, packed, out_sum, sums, bias = layer_call(
         live,
@@ -963,33 +1065,51 @@
         qkv,
         in_weight,
         down_weight,
-        weight_all,
+        *low_weights,
         out_weight,
         context,
         log_total,
         segment,
-        vectors,
+        out_bias,
+        norm1_gain,
+        norm1_shift,
+        in_bias,
+        down_bias,
+        norm2_gain,
+        norm2_shift,
     )
-    query_sum = jnp.concatenate([packed[:, 0:128], packed[:, 384:448]], axis=1)
-    key_sum = jnp.concatenate([packed[:, 128:256], packed[:, 448:512]], axis=1)
-    value_sum = jnp.concatenate([packed[:, 256:384], packed[:, 512:576]], axis=1)
-    query_bias_sum = jnp.concatenate([bias[0, 0:128], bias[0, 384:448]])
-    value_bias_sum = jnp.concatenate([bias[0, 256:384], bias[0, 640:704]])
+
+    def joined(kind):
+        return jnp.concatenate(
+            [
+                packed[128 * kind : 128 * kind + 128],
+                packed[384 + 64 * kind : 448 + 64 * kind],
+            ]
+        ).astype(F32).T
+
+    def joined_bias(kind):
+        return jnp.concatenate(
+            [
+                bias[0, 128 * kind : 128 * kind + 128],
+                bias[0, 384 + 64 * kind : 448 + 64 * kind],
+            ]
+        )
+
     return (
         result,
         input_grad,
-        query_sum,
-        query_bias_sum,
-        key_sum,
-        value_sum,
-        value_bias_sum,
-        out_sum,
+        joined(0),
+        joined_bias(0),
+        joined(1),
+        joined(2),
+        joined_bias(2),
+        out_sum.astype(F32),
         sums[0],
         sums[1],
         sums[2],
-        in_sum,
+        in_sum.astype(F32),
         sums[6],
-        down_sum,
+        down_sum.astype(F32),
         sums[3],
         sums[4],
         sums[5],

time: 272 us -> 242 us (0.89)
  Pallas kernels: 239 us -> 216 us
  local copies, waits for them, and re-layouts: 30.8 us -> 17.2 us
  other arithmetic: 1.44 us -> 7.18 us
    pallas_call x1, Pallas kernels: 204 us -> 181 us  [layer_call(): pl.pallas_call(layer_kernel, in_specs=[smem] + [hbm] * 11 + [vmem] * (2 +...]
    unnamed x39 -> x36, local copies, waits for them, and re-layouts: 20.4 us -> 11.9 us
    another operation x8 -> x0, local copies, waits for them, and re-layouts: 5.47 us -> none  [local(): jnp.stack([out_bias, norm1_gain, norm1_shift, in_bias, down_bias, norm2_g...]
    convert_element_type x0 -> x3, other arithmetic: none -> 4.01 us  [the longest x1 1.58 us: local(): down_sum.astype(F32)]
where the time goes in v1:
time: 242 us; the launch traced here: 241 us
  Pallas kernels  216 us (89%)
  local copies, waits for them, and re-layouts  17.2 us (7%)
  other arithmetic  7.18 us (3%)
    pallas_call x1, Pallas kernels, layer_call(): pl.pallas_call(layer_kernel, in_specs=[smem] + [hbm] * 11 + [vmem] * (2 +...  181 us
    pallas_call x1, Pallas kernels, attend(): pl.pallas_call(attend_kernel, grid_spec=pltpu.PrefetchScalarGridSpec(num_...  34.3 us
    unnamed x36, local copies, waits for them, and re-layouts  11.9 us

profile of v1, /device:TPU:0, one launch (start us, length us, event | category | flops | bytes accessed | tf_op | source)
XLA Modules:
  0.0 240.9 jit_solution(10756607656075829935)
XLA Ops:
  0.7 0.7 compare_convert_fusion.live
  1.3 0.0 copy-start.1
  1.3 1.0 copy-done.1
  2.3 0.0 copy-start.2
  2.3 1.0 copy-done.2
  3.2 0.0 copy-start.3
  3.2 1.0 copy-done.3
  4.2 0.0 copy-start.4
  4.2 1.0 copy-done.4
  5.2 0.0 copy-start.8
  5.2 0.7 copy-done.8
  5.9 0.0 copy-start.10
  5.9 0.7 copy-done.10
  6.5 0.0 copy-start.11
  6.5 0.7 copy-done.11
  7.2 0.0 copy-start.9
  7.2 34.3 %attend.1 = (bf16[2048,768]{1,0:T(8,128)(2,1)S(1)}, f32[16,1024]{1,0:T(8,128)S(1)}, bf16[2048,192]{1,0:T(8,128)(2,1)S(1)}, bf16[2048,768]{1,0:T(8,128)(2,1)}, f32[16,1024]{1,0:T(8,128)S(1)}) custom-call(s32[1]{0:T(128)} %bitcast.place, s32[2]{0:T(128)S(1)} %compare_convert_fusion.live, bf16[2,1024,768]{2,1,0:T(8,128)(2,1)} %token_hbm.1, ...), custom_call_target="tpu_custom_call" | custom-call | tf_op jit(solution)/shard_map/attend/pallas_call | solution.py:143
  41.6 0.0 copy-done.9
  41.6 0.0 copy-start
  41.6 1.7 copy-done
  43.2 0.0 copy-start.5
  43.2 1.0 copy-done.5
  44.2 0.0 copy-start.6
  44.2 0.6 copy-done.6
  44.8 0.0 copy-start.7
  44.8 0.6 copy-done.7
  45.5 181.5 %layer.1 = (bf16[2,256,768]{2,1,0:T(8,128)(2,1)}, f32[2,256,768]{2,1,0:T(8,128)}, bf16[768,768]{1,0:T(8,128)(2,1)}, bf16[768,768]{1,0:T(8,128)(2,1)}, bf16[576,7...) custom-call(s32[2]{0:T(128)} %copy-done.9, ...), custom_call_target="tpu_custom_call" | custom-call | tf_op jit(solution)/shard_map/layer/pallas_call | solution.py:960
  226.9 0.0 copy-start.16
  226.9 0.7 slice_bitcast_fusion.1
  227.7 0.7 slice_bitcast_fusion
  228.4 0.6 pad_maximum_fusion
  228.9 1.7 slice_reduce_fusion
  230.6 1.0 fusion.1
  231.6 0.0 copy-start.14
  231.6 1.3 fusion
  232.9 0.9 convert_bitcast_fusion.2
  233.7 0.0 copy-done.16
  233.7 0.9 convert_element_type.16
  234.6 0.0 copy-start.13
  234.6 1.1 convert_bitcast_fusion
  235.7 0.0 copy-done.14
  235.7 1.6 convert_element_type.17
  237.3 0.0 copy-done.13
  237.3 0.0 copy-start.15
  237.3 0.0 copy-start.12
  237.3 1.6 convert_element_type.18
  238.8 0.0 copy-done.15
  238.8 0.9 copy.38
  239.7 0.0 copy-done.12
  239.8 1.1 copy.39
Async XLA Ops:
  1.3 1.0 copy-start.1
  2.3 1.0 copy-start.2
  3.2 1.0 copy-start.3
  4.2 1.0 copy-start.4
  5.2 0.7 copy-start.8
  5.9 0.7 copy-start.10
  6.5 0.7 copy-start.11
  7.2 34.3 %copy-start.9 = (s32[2]{0:T(128)}, s32[2]{0:T(128)S(1)}, u32[]{:S(2)}) copy-start(s32[2]{0:T(128)S(1)} %compare_convert_fusion.live) | copy-start | bytes 28
  41.6 1.7 copy-start
  43.2 1.0 copy-start.5
  44.2 0.6 copy-start.6
  44.8 0.6 copy-start.7
  226.9 6.8 %copy-start.16 = (bf16[192,768]{1,0:T(8,128)(2,1)S(1)}, bf16[192,768]{1,0:T(8,128)(2,1)}, u32[]{:S(2)}) copy-start(bf16[192,768]{1,0:T(8,128)(2,1)} %get-tuple-element.39) | copy-start | bytes 884740
  231.6 4.1 %copy-start.14 = (bf16[768,768]{1,0:T(8,128)(2,1)S(1)}, bf16[768,768]{1,0:T(8,128)(2,1)}, u32[]{:S(2)}) copy-start(bf16[768,768]{1,0:T(8,128)(2,1)} %get-tuple-element.41) | copy-start | bytes 3538948
  234.6 2.7 %copy-start.13 = (bf16[768,768]{1,0:T(8,128)(2,1)S(1)}, bf16[768,768]{1,0:T(8,128)(2,1)}, u32[]{:S(2)}) copy-start(bf16[768,768]{1,0:T(8,128)(2,1)} %get-tuple-element.42) | copy-start | bytes 3538948
  237.3 1.6 copy-start.15
  237.3 2.5 %copy-start.12 = (f32[2,256,768]{2,1,0:T(8,128)S(1)}, f32[2,256,768]{2,1,0:T(8,128)}, u32[]{:S(2)}) copy-start(f32[2,256,768]{2,1,0:T(8,128)} %get-tuple-element.82) | copy-start | bytes 4718596

commit v2 on v1

--- a/solution.py
+++ b/solution.py
@@ -58,132 +58,6 @@
 
 def column_of(row):
     return jnp.transpose(jnp.broadcast_to(row, (8, row.shape[1])))[:, 0:1]
-
-
-def attend_kernel(
-    place, live, tokens, lengths, query_weight, key_weight, value_weight, query_bias,
-    value_bias, out_weight,
-    qkv, log_total, context, partial, segment,
-    weight, value_t, bias, seg_col,
-):
-    micro, step = pl.program_id(0), pl.program_id(1)
-    rows_all = tokens.shape[1]
-
-    @pl.when((micro == 0) & (step == 0))
-    def _():
-        bias[...] = jnp.zeros_like(bias)
-        for kind, ref in enumerate((query_weight, key_weight, value_weight)):
-            weight[128 * kind : 128 * kind + 128, :] = ref[0:128, :]
-            weight[384 + 128 * kind : 448 + 128 * kind, :] = ref[128:192, :]
-            weight[448 + 128 * kind : 512 + 128 * kind, :] = jnp.zeros_like(ref[128:192, :])
-        for kind, ref in ((0, query_bias), (2, value_bias)):
-            bias[0:1, 128 * kind : 128 * kind + 128] = ref[0:1, 0:128]
-            bias[0:1, 384 + 128 * kind : 448 + 128 * kind] = ref[0:1, 128:192]
-
-    @pl.when(step == 0)
-    def _():
-        def project(index, carry):
-            rows = pl.ds(pl.multiple_of(index * QB, QB), QB)
-            qkv[rows, :] = (
-                back_dot(tokens[0, rows, :], weight[...]) + bias[0:1, :]
-            ).astype(BF)
-            for tile in range(2):
-                value_t[128 * tile : 128 * tile + 128, rows] = jnp.transpose(
-                    qkv[rows, tile_lanes(2, tile)]
-                )
-            return carry
-
-        lax.fori_loop(0, rows_all // QB, project, 0)
-        ends = jnp.broadcast_to(lengths[0], (8, rows_all))
-        lane = lax.broadcasted_iota(jnp.int32, (8, rows_all), 1)
-        shift = 1
-        while shift < rows_all:
-            ends = ends + jnp.where(lane >= shift, pltpu.roll(ends, shift, 1), 0)
-            shift *= 2
-        ends_col = column_of(ends[0:1, :].astype(F32))
-        places = lax.broadcasted_iota(jnp.int32, (rows_all, rows_all), 1).astype(F32)
-        count = jnp.sum(jnp.where(ends_col <= places, 1.0, 0.0), axis=0, keepdims=True)
-        segment[...] = jnp.broadcast_to(count, (8, rows_all))
-        seg_col[...] = column_of(count)
-
-    rows = pl.ds(pl.multiple_of(step * QB, QB), QB)
-    same = seg_col[...] == segment[0:1, rows]
-    outs = []
-    logs = []
-    for head in range(3):
-        tile = head // 2
-        query = qkv[rows, tile_lanes(0, tile)] * jnp.asarray(0.125, BF)
-        query = lane_half(query, head % 2)
-        keys = qkv[:, tile_lanes(1, tile)]
-        scores = jnp.where(same, back_dot(keys, query), -1e30)
-        top = jnp.max(scores, axis=0, keepdims=True)
-        expo = jnp.exp(scores - top)
-        total = jnp.sum(expo, axis=0, keepdims=True)
-        probs = (expo * (1.0 / total)).astype(BF)
-        outs.append(
-            jnp.dot(
-                value_t[64 * head : 64 * head + 64, :], probs, preferred_element_type=F32
-            )
-        )
-        logs.append(top + jnp.log(total))
-    context_t = jnp.concatenate(outs, axis=0) * live[micro].astype(F32)
-    low = jnp.transpose(context_t).astype(BF)
-    context[...] = low
-    log_total[...] = jnp.concatenate(logs + [jnp.zeros((5, QB), F32)], axis=0)
-    partial[...] = jnp.dot(low, out_weight[...], preferred_element_type=F32).astype(BF)
-
-
-def attend(
-    place, live, tokens, lengths, query_weight, key_weight, value_weight, query_bias,
-    value_bias, out_weight,
-):
-    micro_count, rows, width = tokens.shape
-    steps = rows // QB
-    full = lambda array: pl.BlockSpec(array.shape, lambda m, i, *_: (0,) * array.ndim)
-    return pl.pallas_call(
-        attend_kernel,
-        grid_spec=pltpu.PrefetchScalarGridSpec(
-            num_scalar_prefetch=2,
-            grid=(micro_count, steps),
-            in_specs=[
-                pl.BlockSpec((1, rows, width), lambda m, i, *_: (m, 0, 0)),
-                pl.BlockSpec((1, 1, rows), lambda m, i, *_: (m, 0, 0)),
-                full(query_weight),
-                full(key_weight),
-                full(value_weight),
-                full(query_bias),
-                full(value_bias),
-                full(out_weight),
-            ],
-            out_specs=[
-                pl.BlockSpec((rows, 3 * WIDE), lambda m, i, *_: (m, 0)),
-                pl.BlockSpec((8, QB), lambda m, i, *_: (m, i)),
-                pl.BlockSpec((QB, 192), lambda m, i, *_: (m * steps + i, 0)),
-                pl.BlockSpec((QB, width), lambda m, i, p, l: (m * steps + (i ^ p[0]), 0)),
-                pl.BlockSpec((8, rows), lambda m, i, *_: (m, 0)),
-            ],
-            scratch_shapes=[
-                pltpu.VMEM((3 * WIDE, width), BF),
-                pltpu.VMEM((WIDE, rows), BF),
-                pltpu.VMEM((8, 3 * WIDE), F32),
-                pltpu.VMEM((rows, 1), F32),
-            ],
-        ),
-        out_shape=[
-            jax.ShapeDtypeStruct((micro_count * rows, 3 * WIDE), BF),
-            jax.ShapeDtypeStruct((micro_count * 8, rows), F32),
-            jax.ShapeDtypeStruct((micro_count * rows, 192), BF),
-            jax.ShapeDtypeStruct((micro_count * rows, width), BF),
-            jax.ShapeDtypeStruct((micro_count * 8, rows), F32),
-        ],
-        compiler_params=pltpu.CompilerParams(
-            dimension_semantics=("arbitrary", "arbitrary"), vmem_limit_bytes=48 << 20
-        ),
-        name="attend",
-    )(
-        place, live, tokens, lengths, query_weight, key_weight, value_weight, query_bias,
-        value_bias, out_weight,
-    )
 
 
 CHUNK = 48
@@ -422,21 +296,20 @@
 
 
 def layer_kernel(
-    live, partial_hbm, token_hbm, cot_hbm, qkv_hbm, in_hbm, down_hbm, query_hbm, key_hbm,
-    value_hbm, out_hbm, context_hbm, log_total, segment, *rest
+    quarters, token_hbm, cot_hbm, in_hbm, down_hbm, query_hbm, key_hbm, value_hbm, out_hbm,
+    lengths, query_bias, value_bias, *rest
 ):
     layer_body(
-        live, partial_hbm, token_hbm, cot_hbm, qkv_hbm, in_hbm, down_hbm,
-        (query_hbm, key_hbm, value_hbm), out_hbm, context_hbm, log_total, segment,
-        rest[:7], *rest[7:]
+        quarters, token_hbm, cot_hbm, in_hbm, down_hbm, (query_hbm, key_hbm, value_hbm), out_hbm,
+        lengths, query_bias, value_bias, rest[:7], *rest[7:]
     )
 
 
 def layer_body(
-    live, partial_hbm, token_hbm, cot_hbm, qkv_hbm, in_hbm, down_hbm, low_hbm, out_hbm,
-    context_hbm, log_total, segment, vectors,
-    result, input_grad, in_whole, down_whole, qkv_whole, out_whole, sums_out, bias_out,
-    in_weight, down_weight, context,
+    quarters, token_hbm, cot_hbm, in_hbm, down_hbm, low_hbm, out_hbm, lengths, query_bias,
+    value_bias, vectors,
+    result, input_grad, in_whole, down_whole, qkv_whole, out_whole, sums_out, bias_out, qkv_hbm,
+    in_weight, down_weight, context, log_total, segment, low_bias,
     in_term, down_term, qkv_term, out_term, weight_all,
     far, near, cross, sums, hid, gm2, act, slope, gpre, pbuf, grad_low,
     hidden_rows, normed_rows, inverse_rows, key_t, key_acc, value_acc, seg_col, out_wide,
@@ -557,16 +430,23 @@
     def micro_block(micro):
         return pl.ds(micro * rows_all, rows_all)
 
+    def alive_of(micro):
+        return jnp.clip(quarters[micro] - place, 0, 1).astype(F32)
+
     first_row = pl.multiple_of(place * share, share)
-    part_loads = [
-        load(partial_hbm.at[micro_block(m), :], pbuf.at[micro_block(m), :]) for m in range(2)
+    low_loads = [
+        load(ref.at[lanes, :], gpre.at[start + 128 * kind : start + 128 * kind + size, :])
+        for kind, ref in enumerate(low_hbm)
+        for lanes, start, size in ((slice(0, 128), 0, 128), (slice(128, 192), 384, 64))
     ]
+    micro_loads = [load(token_hbm.at[m], act.at[micro_block(m), :]) for m in range(2)]
+    out_load = load(out_hbm, out_wide.at[0:192, :])
     row_loads = [
         load(token_hbm.at[m, pl.ds(first_row, share), :], slot(grad_low, m, 0))
         for m in range(2)
     ] + [load(cot_hbm.at[m, pl.ds(first_row, share), :], result.at[m]) for m in range(2)]
     weight_loads = [load(in_hbm, in_weight), load(down_hbm, down_weight)]
-    late_loads = [load(out_hbm, out_wide.at[0:192, :]), load(context_hbm, context)]
+    late_loads = []
     for kind, ref in enumerate(low_hbm):
         late_loads.append(
             load(ref.at[0:128, :], weight_all.at[128 * kind : 128 * kind + 128, :])
@@ -626,15 +506,7 @@
     weight_all[576:640, :] = jnp.zeros((64, weight_all.shape[1]), BF)
     pl.semaphore_wait(barrier, len(partners))
 
-    for micro in range(2):
-        part_loads[micro].wait()
-        scatter_start(pbuf, micro, 0)
-    for micro in range(2):
-        scatter_mid(pbuf, micro, 0)
-    for handle in row_loads + weight_loads:
-        handle.wait()
-
-    def opening(micro, carry):
+    def opening(micro):
         total = scatter_end(pbuf, micro, 0)
         hidden, normed, inverse = layer_norm(
             slot(grad_low, micro, 0)[...].astype(F32) + total + vector(0), vector(1), vector(2)
@@ -644,11 +516,106 @@
         own_rows(inverse_rows, micro)[...] = jnp.broadcast_to(inverse, (share, 128))
         slot(hid, micro, 0)[...] = hidden.astype(BF)
         gather_start(hid, micro, 0)
+
+    low_bias[...] = jnp.zeros_like(low_bias)
+    for kind, ref in ((0, query_bias), (2, value_bias)):
+        row = ref[...].reshape(1, -1)
+        low_bias[0:1, 128 * kind : 128 * kind + 128] = row[:, 0:128]
+        low_bias[0:1, 384 + 128 * kind : 448 + 128 * kind] = row[:, 128:192]
+    for kind in range(3):
+        gpre[448 + 128 * kind : 512 + 128 * kind, :] = jnp.zeros((64, gpre.shape[1]), BF)
+    for handle in low_loads + micro_loads + [out_load] + row_loads:
+        handle.wait()
+    qkv, value_t = gm2, key_t
+
+    def project(micro):
+        def one(index, carry):
+            at = pl.multiple_of(index * share, share)
+            rows = pl.ds(pl.multiple_of(micro * rows_all + index * share, share), share)
+            qkv[rows, :] = (back_dot(act[rows, :], gpre[0:768, :]) + low_bias[0:1, :]).astype(BF)
+            for tile in range(2):
+                value_t[128 * tile : 128 * tile + 128, pl.ds(at, share)] = jnp.transpose(
+                    qkv[rows, tile_lanes(2, tile)]
+                )
+            return carry
+
+        lax.fori_loop(0, 4, one, 0)
+        ends = jnp.broadcast_to(lengths[micro], (8, rows_all))
+        lane = lax.broadcasted_iota(jnp.int32, (8, rows_all), 1)
+        shift = 1
+        while shift < rows_all:
+            ends = ends + jnp.where(lane >= shift, pltpu.roll(ends, shift, 1), 0)
+            shift *= 2
+        ends_col = column_of(ends[0:1, :].astype(F32))
+        places = lax.broadcasted_iota(jnp.int32, (rows_all, rows_all), 1).astype(F32)
+        count = jnp.sum(jnp.where(ends_col <= places, 1.0, 0.0), axis=0, keepdims=True)
+        segment[pl.ds(pl.multiple_of(micro * 8, 8), 8), :] = jnp.broadcast_to(count, (8, rows_all))
+        seg_col[...] = column_of(count)
+
+    def attend(index, carry):
+        micro, turn = index // 4, index % 4
+        which = 3 - turn
+
+        @pl.when(turn == 0)
+        def _():
+            project(micro)
+
+        step = which ^ place
+        block = pl.ds(pl.multiple_of(micro * rows_all, rows_all), rows_all)
+        rows = pl.ds(pl.multiple_of(micro * rows_all + step * share, share), share)
+        eight = pl.ds(pl.multiple_of(micro * 8, 8), 8)
+        columns = pl.ds(pl.multiple_of(step * share, share), share)
+        same = seg_col[...] == segment[eight, columns][0:1, :]
+        outs = []
+        logs = []
+        for head in range(3):
+            tile = head // 2
+            query = qkv[rows, tile_lanes(0, tile)] * jnp.asarray(0.125, BF)
+            query = lane_half(query, head % 2)
+            keys = qkv[block, tile_lanes(1, tile)]
+            scores = jnp.where(same, back_dot(keys, query), -1e30)
+            top = jnp.max(scores, axis=0, keepdims=True)
+            expo = jnp.exp(scores - top)
+            total = jnp.sum(expo, axis=0, keepdims=True)
+            probs = (expo * (1.0 / total)).astype(BF)
+            outs.append(
+                jnp.dot(
+                    value_t[64 * head : 64 * head + 64, :], probs, preferred_element_type=F32
+                )
+            )
+            logs.append(top + jnp.log(total))
+        context_t = jnp.concatenate(outs, axis=0) * alive_of(micro)
+        low = jnp.transpose(context_t).astype(BF)
+        context[rows, :] = low
+        log_total[eight, columns] = jnp.concatenate(logs + [jnp.zeros((5, share), F32)], axis=0)
+        slot(pbuf, micro, which)[...] = jnp.dot(
+            low, out_wide[0:192, :], preferred_element_type=F32
+        ).astype(BF)
+
+        @pl.when(turn == 0)
+        def _():
+            far_copy(pbuf, micro, 0).start()
+
+        @pl.when(turn == 1)
+        def _():
+            scatter_mid(pbuf, micro, 0)
+
+        @pl.when(turn == 2)
+        def _():
+            near_copy(pbuf, micro, 0).start()
+
+        @pl.when(index == 4)
+        def _():
+            opening(0)
+
         return carry
 
-    lax.fori_loop(0, 2, opening, 0)
-    for micro in range(2):
-        scatter_drain(pbuf, micro, 0)
+    lax.fori_loop(0, 8, attend, 0)
+    qkv_store = load(gm2, qkv_hbm)
+    for handle in weight_loads:
+        handle.wait()
+    scatter_drain(pbuf, 0, 0)
+    scatter_drain(pbuf, 1, 0)
 
     def forward(index, carry):
         micro, which = index // 4, index % 4
@@ -657,7 +624,7 @@
             jnp.dot(slot(hid, micro, which)[...], in_weight[...], preferred_element_type=F32)
             + vector(3)
         )
-        alive = live[micro].astype(F32)
+        alive = alive_of(micro)
         below = 0.5 * (1.0 + lax.erf(pre * ROOT_HALF)) * alive
         low = (pre * below).astype(BF)
         slot(act, micro, which)[...] = low
@@ -671,6 +638,11 @@
         @pl.when(which == 3)
         def _():
             scatter_start(pbuf, micro, 1)
+
+        @pl.when(index == 1)
+        def _():
+            opening(1)
+            qkv_store.wait()
 
         @pl.when(index == 4)
         def _():
@@ -848,7 +820,7 @@
         def _():
             named["o0"].advance(0)
 
-        alive = live[micro].astype(BF)
+        alive = alive_of(micro).astype(BF)
         grad_context = back_dot(grad_slot, out_wide[...]).astype(BF) * alive
         same = seg_col[...] == seg_row
         query_parts = []
@@ -943,8 +915,8 @@
 
 
 def layer_call(
-    live, partials, tokens, cotangent, qkv, in_weight, down_weight, query_weight, key_weight,
-    value_weight, out_weight, context, log_total, segment, *vectors
+    quarters, tokens, cotangent, in_weight, down_weight, query_weight, key_weight, value_weight,
+    out_weight, lengths, query_bias, value_bias, *vectors
 ):
     micro_count, rows_all, width = tokens.shape
     share = rows_all // 4
@@ -959,8 +931,8 @@
     batch_sems = 14 * 2 * batch_bits + 2
     return pl.pallas_call(
         layer_kernel,
-        in_specs=[smem] + [hbm] * 11 + [vmem] * (2 + len(vectors)),
-        out_specs=[vmem] * 8,
+        in_specs=[smem] + [hbm] * 8 + [vmem] * (3 + len(vectors)),
+        out_specs=[vmem] * 8 + [hbm],
         out_shape=[
             jax.ShapeDtypeStruct((micro_count, share, width), BF),
             jax.ShapeDtypeStruct((micro_count, share, width), F32),
@@ -970,11 +942,15 @@
             jax.ShapeDtypeStruct((192, width), BF),
             jax.ShapeDtypeStruct((8, width), F32),
             jax.ShapeDtypeStruct((8, width), F32),
+            jax.ShapeDtypeStruct((rows, 3 * WIDE), BF),
         ],
         scratch_shapes=[
             pltpu.VMEM((width, units), BF),
             pltpu.VMEM((units, width), BF),
             pltpu.VMEM((rows, 192), BF),
+            pltpu.VMEM((8 * micro_count, rows_all), F32),
+            pltpu.VMEM((8 * micro_count, rows_all), F32),
+            pltpu.VMEM((8, 3 * WIDE), F32),
             pltpu.VMEM((width, units), F32),
             pltpu.VMEM((units, width), F32),
             pltpu.VMEM((576, width), F32),
@@ -1011,15 +987,15 @@
             pltpu.SemaphoreType.DMA((48,)),
             pltpu.SemaphoreType.DMA((batch_sems,)),
             pltpu.SemaphoreType.DMA((batch_sems,)),
-            pltpu.SemaphoreType.DMA((20,)),
+            pltpu.SemaphoreType.DMA((32,)),
         ],
         compiler_params=pltpu.CompilerParams(
             collective_id=1, has_side_effects=True, vmem_limit_bytes=67_043_328
         ),
         name="layer",
     )(
-        live, partials, tokens, cotangent, qkv, in_weight, down_weight, query_weight,
-        key_weight, value_weight, out_weight, context, log_total, segment, *vectors
+        quarters, tokens, cotangent, in_weight, down_weight, query_weight, key_weight,
+        value_weight, out_weight, lengths, query_bias, value_bias, *vectors
     )
 
 
@@ -1044,32 +1020,19 @@
     norm2_shift,
     cotangent,
 ):
-    place = lax.axis_index("tensor").astype(jnp.int32)
-    live = (4 * place < 4 * quarters).astype(jnp.int32)
-    low_weights = (query_weight.T, key_weight.T, value_weight.T)
-    qkv, log_total, context, partials, segment = attend(
-        place[None],
-        live,
-        tokens,
-        lengths.reshape(lengths.shape[0], 1, lengths.shape[2]),
-        *low_weights,
-        query_bias[None],
-        value_bias[None],
-        out_weight,
-    )
-    result, input_grad, in_sum, down_sum, packed, out_sum, sums, bias = layer_call(
-        live,
-        partials,
+    result, input_grad, in_sum, down_sum, packed, out_sum, sums, bias, _ = layer_call(
+        quarters,
         tokens,
         cotangent,
-        qkv,
         in_weight,
         down_weight,
-        *low_weights,
+        query_weight.T,
+        key_weight.T,
+        value_weight.T,
         out_weight,
-        context,
-        log_total,
-        segment,
+        lengths.reshape(lengths.shape[0], 1, lengths.shape[2]),
+        query_bias,
+        value_bias,
         out_bias,
         norm1_gain,
         norm1_shift,

time: 242 us -> 213 us (0.88)
  Pallas kernels: 216 us -> 196 us
  local copies, waits for them, and re-layouts: 17.2 us -> 8.26 us
    pallas_call x2 -> x1, Pallas kernels: 216 us -> 196 us  [layer_call(): pl.pallas_call(layer_kernel, in_specs=[smem] + [hbm] * 8 + [vmem] * (3 +...]
    unnamed x36 -> x12, local copies, waits for them, and re-layouts: 11.9 us -> 2.94 us
where the time goes in v2:
time: 213 us; the launch traced here: 211 us
  Pallas kernels  196 us (92%)
  local copies, waits for them, and re-layouts  8.26 us (4%)
  other arithmetic  6.52 us (3%)
    pallas_call x1, Pallas kernels, layer_call(): pl.pallas_call(layer_kernel, in_specs=[smem] + [hbm] * 8 + [vmem] * (3 +...  196 us

profile of v2, /device:TPU:0, one launch (start us, length us, event | category | flops | bytes accessed | tf_op | source)
XLA Modules:
  0.0 211.4 jit_solution(12268393260114831654)
XLA Ops:
  0.7 195.9 %layer.1 = (bf16[2,256,768]{2,1,0:T(8,128)(2,1)}, f32[2,256,768]{2,1,0:T(8,128)}, bf16[768,768]{1,0:T(8,128)(2,1)}, bf16[768,768]{1,0:T(8,128)(2,1)}, bf16[576,7...) custom-call(s32[2]{0:T(128)} %quarters.1, ...), custom_call_target="tpu_custom_call" | custom-call | tf_op jit(solution)/shard_map/layer/pallas_call | solution.py:932
  196.6 0.0 copy-start.4
  196.6 0.7 slice_bitcast_fusion.1
  197.3 0.7 slice_bitcast_fusion
  198.0 0.6 pad_maximum_fusion
  198.5 1.7 slice_reduce_fusion
  200.3 1.0 fusion.1
  201.3 1.2 fusion
  202.5 0.0 copy-start.2
  202.5 0.9 convert_bitcast_fusion.2
  203.3 0.0 copy-done.4
  203.3 0.9 convert_element_type.12
  204.2 1.1 convert_bitcast_fusion
  205.3 0.0 copy-done.2
  205.3 0.0 copy-start.1
  205.3 1.6 convert_element_type.13
  206.9 0.1 copy-done.1
  207.0 0.0 copy-start.3
  207.0 1.6 convert_element_type.14
  208.5 0.0 copy-done.3
  208.5 0.0 copy-start
  208.5 0.9 copy.38
  209.4 0.8 copy-done
  210.2 1.1 copy.39
Async XLA Ops:
  196.6 6.8 %copy-start.4 = (bf16[192,768]{1,0:T(8,128)(2,1)S(1)}, bf16[192,768]{1,0:T(8,128)(2,1)}, u32[]{:S(2)}) copy-start(bf16[192,768]{1,0:T(8,128)(2,1)} %get-tuple-element.29) | copy-start | bytes 884740
  202.5 2.8 %copy-start.2 = (bf16[768,768]{1,0:T(8,128)(2,1)S(1)}, bf16[768,768]{1,0:T(8,128)(2,1)}, u32[]{:S(2)}) copy-start(bf16[768,768]{1,0:T(8,128)(2,1)} %get-tuple-element.31) | copy-start | bytes 3538948
  205.3 1.7 copy-start.1
  207.0 1.6 copy-start.3
  208.5 1.7 copy-start

commit v3 on v2

--- a/solution.py
+++ b/solution.py
@@ -232,66 +232,38 @@
 
 
 EVENTS = {
-    "open": (
-        "d0", "d2",
-    ),
-    "closing": (
-        "d1", "d3",
-    ),
-    "closed": (
-        "s",
-    ),
-    0: (
-        "d0", "d2", "i0", "d1",
-    ),
-    1: (
-        "s", "d3", "i1",
-    ),
-    2: (
-        "i0", "i2", "d2", "i3",
-    ),
-    3: (
-        "s", "i1", "d3", "d0", "d1", "i2",
-    ),
-    "between": (
-        "i0", "d2", "i3",
-    ),
-    "weighed": (
-        "i1",
-    ),
-    4: (
-        "d3", "d2", "d0",
-    ),
-    5: (
-        "s", "d1",
-    ),
-    6: (
-        "s", "d3", "i0", "i2",
-    ),
-    7: (
-        "s", "i1", "i3", "d0",
-    ),
-    "start": (
-        "i0", "d1",
-    ),
-    "pre": (
-        "i1", "i2",
-    ),
-    "mid": (
-        "q0",
-    ),
-    "tail": (
-        "o0", "i3", "q1", "q0", "o0", "q2", "q1", "q0",
-    ),
+    "closing": ("d0",),
+    1: ("i1", "d1",),
+    3: ("i3", "d2",),
+    4: ("d0",),
+    "closed": ("s", "d3", "i1", "d1",),
+    7: ("i0", "i3",),
+    8: ("d2",),
+    9: ("s", "i2", "d0", "d3",),
+    10: ("i1",),
+    11: ("i3", "d1",),
+    12: ("s", "i0",),
+    13: ("d2",),
+    14: ("i2",),
+    15: ("s", "d0",),
+    17: ("d3",),
+    "between": ("i1", "d0", "i3", "d1",),
+    18: ("s", "i0", "d2",),
+    20: ("d1", "i2",),
+    21: ("s", "d3",),
+    22: ("d2", "i1",),
+    "start": ("i3", "d3",),
+    "pre": ("i0", "i2",),
+    "tail": ("q0", "o0", "q1", "q0", "o0", "q2", "q1",),
     "end": (
-        "i2", "q2", "q1", "i3", "q0", "o0", "q2", "q1", "q0", "o0",
-        "q2", "q1", "o0", "q2",
+        "q0", "i0", "q2", "q1", "i2", "q0", "o0", "q2", "q1", "q0",
+        "q2", "o0", "q1", "q2", "o0",
     ),
 }
-Z_FIRST = ("d0", "d1", "o0",)
+Z_FIRST = ("i1", "i3", "o0",)
 POINTS = (
-    "open", "closing", "closed", 0, 1, 2, 3, "between", "weighed", 4, 5, 6, 7,
-    "start", "pre", "mid", "tail", "end",
+    "open", "closing", *range(6), "closed", *range(6, 18), "between", "weighed",
+    *range(18, 24), "start", "pre", "mid", "tail", "end",
 )
 
 
@@ -312,7 +284,7 @@
     in_weight, down_weight, context, log_total, segment, low_bias,
     in_term, down_term, qkv_term, out_term, weight_all,
     far, near, cross, sums, hid, gm2, act, slope, gpre, pbuf, grad_low,
-    hidden_rows, normed_rows, inverse_rows, key_t, key_acc, value_acc, seg_col, out_wide,
+    hidden_rows, normed_rows, inverse_rows, key_t, key_acc, value_acc, out_wide,
     down_take, in_take, qkv_take, out_take, vec_values, vec_take, bias_values, bias_take,
     send_sem, recv_sem, batch_send, batch_recv, load_sem,
 ):
@@ -504,7 +476,6 @@
     out_term[...] = jnp.zeros_like(out_term)
     out_wide[192:256, :] = jnp.zeros((64, out_wide.shape[1]), BF)
     weight_all[576:640, :] = jnp.zeros((64, weight_all.shape[1]), BF)
-    pl.semaphore_wait(barrier, len(partners))
 
     def opening(micro):
         total = scatter_end(pbuf, micro, 0)
@@ -524,7 +495,22 @@
         low_bias[0:1, 384 + 128 * kind : 448 + 128 * kind] = row[:, 128:192]
     for kind in range(3):
         gpre[448 + 128 * kind : 512 + 128 * kind, :] = jnp.zeros((64, gpre.shape[1]), BF)
-    for handle in low_loads + micro_loads + [out_load] + row_loads:
+    def find_segments(micro, carry):
+        ends = jnp.broadcast_to(lengths[micro], (8, rows_all))
+        lane = lax.broadcasted_iota(jnp.int32, (8, rows_all), 1)
+        shift = 1
+        while shift < rows_all:
+            ends = ends + jnp.where(lane >= shift, pltpu.roll(ends, shift, 1), 0)
+            shift *= 2
+        ends_col = column_of(ends[0:1, :].astype(F32))
+        places = lax.broadcasted_iota(jnp.int32, (rows_all, rows_all), 1).astype(F32)
+        count = jnp.sum(jnp.where(ends_col <= places, 1.0, 0.0), axis=0, keepdims=True)
+        segment[pl.ds(pl.multiple_of(micro * 8, 8), 8), :] = jnp.broadcast_to(count, (8, rows_all))
+        return carry
+
+    lax.fori_loop(0, 2, find_segments, 0)
+    pl.semaphore_wait(barrier, len(partners))
+    for handle in low_loads + [micro_loads[0], out_load]:
         handle.wait()
     qkv, value_t = gm2, key_t
 
@@ -540,32 +526,31 @@
             return carry
 
         lax.fori_loop(0, 4, one, 0)
-        ends = jnp.broadcast_to(lengths[micro], (8, rows_all))
-        lane = lax.broadcasted_iota(jnp.int32, (8, rows_all), 1)
-        shift = 1
-        while shift < rows_all:
-            ends = ends + jnp.where(lane >= shift, pltpu.roll(ends, shift, 1), 0)
-            shift *= 2
-        ends_col = column_of(ends[0:1, :].astype(F32))
-        places = lax.broadcasted_iota(jnp.int32, (rows_all, rows_all), 1).astype(F32)
-        count = jnp.sum(jnp.where(ends_col <= places, 1.0, 0.0), axis=0, keepdims=True)
-        segment[pl.ds(pl.multiple_of(micro * 8, 8), 8), :] = jnp.broadcast_to(count, (8, rows_all))
-        seg_col[...] = column_of(count)
 
     def attend(index, carry):
         micro, turn = index // 4, index % 4
         which = 3 - turn
 
+        @pl.when(index == 4)
+        def _():
+            micro_loads[1].wait()
+
         @pl.when(turn == 0)
         def _():
             project(micro)
+
+        @pl.when(index == 4)
+        def _():
+            for handle in row_loads:
+                handle.wait()
+            opening(0)
 
         step = which ^ place
         block = pl.ds(pl.multiple_of(micro * rows_all, rows_all), rows_all)
         rows = pl.ds(pl.multiple_of(micro * rows_all + step * share, share), share)
         eight = pl.ds(pl.multiple_of(micro * 8, 8), 8)
         columns = pl.ds(pl.multiple_of(step * share, share), share)
-        same = seg_col[...] == segment[eight, columns][0:1, :]
+        same = column_of(segment[eight, :][0:1, :]) == segment[eight, columns][0:1, :]
         outs = []
         logs = []
         for head in range(3):
@@ -604,10 +589,6 @@
         def _():
             near_copy(pbuf, micro, 0).start()
 
-        @pl.when(index == 4)
-        def _():
-            opening(0)
-
         return carry
 
     lax.fori_loop(0, 8, attend, 0)
@@ -617,8 +598,37 @@
     scatter_drain(pbuf, 0, 0)
     scatter_drain(pbuf, 1, 0)
 
+    def middle(micro):
+        total = scatter_end(pbuf, micro, 1)
+        final, normed, inverse = layer_norm(
+            own_rows(hidden_rows, micro)[...] + total + vector(4), vector(5), vector(6)
+        )
+        grad_y = result[micro].astype(F32)
+        result[micro] = final.astype(BF)
+        grad_mid2 = norm_back(grad_y, normed, inverse, vector(5))
+        own_rows(hidden_rows, micro)[...] = grad_mid2
+        slot(gm2, micro, 0)[...] = grad_mid2.astype(BF)
+        gather_start(gm2, micro, 1)
+        tally(3, grad_mid2)
+        tally(4, grad_y * normed)
+        tally(5, grad_y)
+
     def forward(index, carry):
         micro, which = index // 4, index % 4
+
+        @pl.when(index == 1)
+        def _():
+            qkv_store.wait()
+
+        @pl.when(index == 4)
+        def _():
+            scatter_mid(pbuf, 0, 1)
+            opening(1)
+
+        @pl.when(index == 6)
+        def _():
+            middle(0)
+
         gather_step(hid, micro, 0, which)
         pre = (
             jnp.dot(slot(hid, micro, which)[...], in_weight[...], preferred_element_type=F32)
@@ -639,42 +649,37 @@
         def _():
             scatter_start(pbuf, micro, 1)
 
-        @pl.when(index == 1)
-        def _():
-            opening(1)
-            qkv_store.wait()
-
-        @pl.when(index == 4)
-        def _():
-            scatter_mid(pbuf, 0, 1)
-
         return carry
 
     lax.fori_loop(0, 8, forward, 0)
     scatter_mid(pbuf, 1, 1)
-
-    def middle(micro, carry):
-        total = scatter_end(pbuf, micro, 1)
-        final, normed, inverse = layer_norm(
-            own_rows(hidden_rows, micro)[...] + total + vector(4), vector(5), vector(6)
-        )
-        grad_y = result[micro].astype(F32)
-        result[micro] = final.astype(BF)
-        grad_mid2 = norm_back(grad_y, normed, inverse, vector(5))
-        own_rows(hidden_rows, micro)[...] = grad_mid2
-        slot(gm2, micro, 0)[...] = grad_mid2.astype(BF)
-        gather_start(gm2, micro, 1)
-        tally(3, grad_mid2)
-        tally(4, grad_y * normed)
-        tally(5, grad_y)
-        return carry
-
-    lax.fori_loop(0, 2, middle, 0)
-    for micro in range(2):
-        scatter_drain(pbuf, micro, 1)
+    scatter_drain(pbuf, 0, 1)
+
+    def weigh(left, right, out, micro):
+        rows = micro_block(micro)
+
+        def block(index, carry):
+            lanes = pl.ds(pl.multiple_of(index * 256, 256), 256)
+            value = cross_dot(left[rows, lanes], right[rows, :])
+            if micro == 0:
+                out[lanes, :] = value
+            else:
+                out[lanes, :] += value
+            return carry
+
+        lax.fori_loop(0, out.shape[0] // 256, block, 0)
 
     def backward(index, carry):
         micro, which = index // 4, index % 4
+
+        @pl.when(index == 4)
+        def _():
+            middle(1)
+            scatter_drain(pbuf, 1, 1)
+            scatter_mid(pbuf, 0, 2)
+            weigh(act, gm2, down_term, 0)
+            weigh(hid, gpre, in_term, 0)
+
         gather_step(gm2, micro, 1, which)
         grad_pre = (
             back_dot(slot(gm2, micro, which)[...], down_weight[...])
@@ -688,26 +693,14 @@
         def _():
             scatter_start(pbuf, micro, 2)
 
-        @pl.when(index == 4)
-        def _():
-            scatter_mid(pbuf, 0, 2)
-
         return carry
 
     lax.fori_loop(0, 8, backward, 0)
-    scatter_mid(pbuf, 1, 2)
-
-    def weigh(left, right, out):
-        def block(index, carry):
-            lanes = pl.ds(pl.multiple_of(index * 256, 256), 256)
-            out[lanes, :] = cross_dot(left[:, lanes], right[...])
-            return carry
-
-        lax.fori_loop(0, out.shape[0] // 256, block, 0)
-
-    weigh(act, gm2, down_term)
+
+    weigh(act, gm2, down_term, 1)
     for k in range(4):
         named["d" + str(k)].advance(0)
+    scatter_mid(pbuf, 1, 2)
     for micro in range(2):
         gather_drain(hid, micro, 0)
         gather_drain(gm2, micro, 1)
@@ -715,7 +708,7 @@
         load(token_hbm.at[m], act.at[micro_block(m), :]) for m in range(2)
     )
     late_loads.append(load(qkv_hbm, gm2))
-    weigh(hid, gpre, in_term)
+    weigh(hid, gpre, in_term, 1)
     for k in range(4):
         named["i" + str(k)].advance(0)
 
@@ -746,14 +739,10 @@
             (shared_sum if name == "s" else named[name]).advance(step)
 
     run("open")
+    for handle in late_loads:
+        handle.wait()
     closing(0)
     run("closing")
-    closing(1)
-    for micro in range(2):
-        scatter_drain(pbuf, micro, 2)
-    run("closed")
-    for handle in late_loads:
-        handle.wait()
     qkv, tokens, grads = gm2, act, gpre
 
     def micro_rows(micro):
@@ -761,10 +750,10 @@
 
     def finish_grads(micro):
         block = micro_block(micro)
-        grads[block, 128:256] = key_acc[:, 0:128].astype(BF)
-        grads[block, 256:384] = value_acc[:, 0:128].astype(BF)
-        grads[block, 448:512] = key_acc[:, 128:192].astype(BF)
-        grads[block, 512:640] = value_acc[:, 128:256].astype(BF)
+        grads[block, 128:256] = key_acc[block, 0:128].astype(BF)
+        grads[block, 256:384] = value_acc[block, 0:128].astype(BF)
+        grads[block, 448:512] = key_acc[block, 128:192].astype(BF)
+        grads[block, 512:640] = value_acc[block, 128:256].astype(BF)
         bias_values[0:1, 0:640] += jnp.sum(
             grads[block, 0:640].astype(F32), axis=0, keepdims=True
         )
@@ -790,24 +779,30 @@
         lax.fori_loop(0, 4, send_slot, 0)
         scatter_start(pbuf, micro, 3)
 
+    def progress(index, head):
+        for turn in range(8):
+            if planned[3 * turn + head]:
+
+                @pl.when(index == turn)
+                def _():
+                    run(3 * turn + head)
+
     def attend_back(index, carry):
-        micro, which = index // 4, index % 4
+        micro, which = (index // 2) % 2, (index // 4) * 2 + index % 2
         gather_step(grad_low, micro, 2, which)
         step = which ^ place
         block = micro_rows(micro)
         rows = pl.ds(pl.multiple_of(micro * rows_all + step * share, share), share)
+        key_at = pl.multiple_of(micro * WIDE, WIDE)
 
         @pl.when(which == 0)
         def _():
             for tile in range(2):
-                key_t[128 * tile : 128 * tile + 128, :] = jnp.transpose(
+                key_t[pl.ds(pl.multiple_of(key_at + 128 * tile, 128), 128), :] = jnp.transpose(
                     qkv[block, tile_lanes(1, tile)]
                 )
-            key_acc[...] = jnp.zeros_like(key_acc)
-            value_acc[...] = jnp.zeros_like(value_acc)
-            seg_col[...] = column_of(
-                segment[pl.ds(pl.multiple_of(micro * 8, 8), 8), :][0:1, :]
-            )
+            key_acc[block, :] = jnp.zeros((rows_all, WIDE), F32)
+            value_acc[block, :] = jnp.zeros((rows_all, WIDE), F32)
 
         eight = pl.ds(pl.multiple_of(micro * 8, 8), 8)
         columns = pl.ds(pl.multiple_of(step * share, share), share)
@@ -822,7 +817,7 @@
 
         alive = alive_of(micro).astype(BF)
         grad_context = back_dot(grad_slot, out_wide[...]).astype(BF) * alive
-        same = seg_col[...] == seg_row
+        same = column_of(segment[eight, :][0:1, :]) == seg_row
         query_parts = []
         for head in range(3):
             tile = head // 2
@@ -837,38 +832,42 @@
             grad_probs = back_dot(values, grad_tile)
             mean = jnp.sum(probs * grad_probs, axis=0, keepdims=True)
             grad_scores = (probs * (grad_probs - mean)).astype(BF)
-            value_acc[:, lanes] += jnp.dot(
+            value_acc[block, lanes] += jnp.dot(
                 probs.astype(BF), grad_tile, preferred_element_type=F32
             )
-            key_acc[:, lanes] += jnp.dot(grad_scores, query, preferred_element_type=F32)
+            key_acc[block, lanes] += jnp.dot(grad_scores, query, preferred_element_type=F32)
             query_parts.append(
                 jnp.dot(
-                    key_t[64 * head : 64 * head + 64, :],
+                    key_t[pl.ds(pl.multiple_of(key_at + 64 * head, 64), 64), :],
                     grad_scores,
                     preferred_element_type=F32,
                 )
             )
+            if head < 2:
+                progress(index, head)
         query_t = jnp.concatenate(query_parts + [jnp.zeros((64, share), F32)], axis=0) * 0.125
         query_grad = jnp.transpose(query_t).astype(BF)
         grads[rows, 0:128] = query_grad[:, 0:128]
         grads[rows, 384:448] = query_grad[:, 128:192]
 
-        for point in range(8):
-            if planned[point]:
-
-                @pl.when(index == point)
-                def _():
-                    run(point)
-
-        @pl.when(index == 3)
-        def _():
+        progress(index, 2)
+
+        @pl.when(index == 1)
+        def _():
+            closing(1)
+            run("closed")
+
+        @pl.when(index == 5)
+        def _():
+            for micro in range(2):
+                scatter_drain(pbuf, micro, 2)
             finish_grads(0)
             send_input(0)
             run("between")
             weigh_low(0)
             run("weighed")
 
-        @pl.when(index == 4)
+        @pl.when(index == 6)
         def _():
             scatter_mid(pbuf, 0, 3)
 
@@ -970,10 +969,9 @@
             pltpu.VMEM((2 * share, width), F32),
             pltpu.VMEM((2 * share, width), F32),
             pltpu.VMEM((2 * share, 128), F32),
-            pltpu.VMEM((WIDE, rows_all), BF),
-            pltpu.VMEM((rows_all, WIDE), F32),
-            pltpu.VMEM((rows_all, WIDE), F32),
-            pltpu.VMEM((rows_all, 1), F32),
+            pltpu.VMEM((micro_count * WIDE, rows_all), BF),
+            pltpu.VMEM((rows, WIDE), F32),
+            pltpu.VMEM((rows, WIDE), F32),
             pltpu.VMEM((WIDE, width), BF),
             pltpu.VMEM((4 * small, width), BF),
             pltpu.VMEM((4 * small, width), BF),
@@ -997,6 +995,100 @@
         quarters, tokens, cotangent, in_weight, down_weight, query_weight, key_weight,
         value_weight, out_weight, lengths, query_bias, value_bias, *vectors
     )
+
+
+def finish_kernel(
+    result_in, grad_in, in_low, down_low, packed, out_low, sums, bias,
+    result, input_grad, query, query_bias, key, value, value_bias, out, out_bias, gain1, shift1,
+    in_out, in_bias, down, down_bias, gain2, shift2,
+    result_buf, grad_buf, in_buf, down_buf, packed_buf, out_buf, in_wide, down_wide, packed_wide,
+    out_wide, sems,
+):
+    taken = []
+
+    def move(src, dst):
+        taken.append(0)
+        handle = pltpu.make_async_copy(src, dst, sems.at[len(taken) - 1])
+        handle.start()
+        return handle
+
+    inner = out_low.shape[0]
+    low = (
+        (in_low, in_buf, in_wide, ((0, in_low.shape[0], in_out, 0),)),
+        (down_low, down_buf, down_wide, ((0, down_low.shape[0], down, 0),)),
+        (
+            packed, packed_buf, packed_wide,
+            tuple(
+                part
+                for kind, ref in enumerate((query, key, value))
+                for part in ((128 * kind, 128, ref, 0), (384 + 64 * kind, 64, ref, 128))
+            ),
+        ),
+        (out_low, out_buf, out_wide, ((0, inner, out, 0),)),
+    )
+    loads = [move(src, buf) for src, buf, _, _ in low]
+    through = [(move(grad_in, grad_buf), grad_buf, input_grad)]
+    through.append((move(result_in, result_buf), result_buf, result))
+    stores = []
+    for load, (_, buf, wide, parts) in zip(loads, low):
+        load.wait()
+        wide[...] = buf[...].astype(F32)
+        for start, size, ref, at in parts:
+            stores.append(move(wide.at[start : start + size, :], ref.at[at : at + size, :]))
+    for load, buf, ref in through:
+        load.wait()
+        stores.append(move(buf, ref))
+    for index, ref in ((0, out_bias), (1, gain1), (2, shift1), (3, down_bias), (4, gain2), (5, shift2), (6, in_bias)):
+        ref[...] = sums[index, :]
+    for kind, ref in ((0, query_bias), (2, value_bias)):
+        row = bias[0:1, 128 * kind : 128 * kind + 128]
+        tail = bias[0:1, 384 + 64 * kind : 448 + 64 * kind]
+        ref[...] = jnp.concatenate([row, tail], axis=1).reshape(inner)
+    for store in stores:
+        store.wait()
+
+
+def finish(result, input_grad, in_sum, down_sum, packed, out_sum, sums, bias):
+    width, units = in_sum.shape
+    inner = out_sum.shape[0]
+    hbm = pl.BlockSpec(memory_space=pl.ANY)
+    vmem = pl.BlockSpec(memory_space=pltpu.VMEM)
+    shape = jax.ShapeDtypeStruct
+    wide = shape((inner, width), F32)
+    row = shape((width,), F32)
+    short = shape((inner,), F32)
+    outs = pl.pallas_call(
+        finish_kernel,
+        in_specs=[hbm] * 6 + [vmem] * 2,
+        out_specs=[
+            hbm, hbm, hbm, vmem, hbm, hbm, vmem, hbm, vmem, vmem, vmem, hbm, vmem, hbm, vmem,
+            vmem, vmem,
+        ],
+        out_shape=[
+            shape(result.shape, BF), shape(input_grad.shape, F32), wide, short, wide, wide,
+            short, wide, row, row, row, shape((width, units), F32), shape((units,), F32),
+            shape((units, width), F32), row, row, row,
+        ],
+        scratch_shapes=[
+            pltpu.VMEM(result.shape, BF),
+            pltpu.VMEM(input_grad.shape, F32),
+            pltpu.VMEM(in_sum.shape, BF),
+            pltpu.VMEM(down_sum.shape, BF),
+            pltpu.VMEM(packed.shape, BF),
+            pltpu.VMEM(out_sum.shape, BF),
+            pltpu.VMEM(in_sum.shape, F32),
+            pltpu.VMEM(down_sum.shape, F32),
+            pltpu.VMEM(packed.shape, F32),
+            pltpu.VMEM(out_sum.shape, F32),
+            pltpu.SemaphoreType.DMA((18,)),
+        ],
+        compiler_params=pltpu.CompilerParams(vmem_limit_bytes=67_043_328),
+        name="finish",
+    )(result, input_grad, in_sum, down_sum, packed, out_sum, sums, bias)
+    outs = list(outs)
+    for index in (2, 4, 5):
+        outs[index] = outs[index].T
+    return tuple(outs)
 
 
 def local(
@@ -1042,41 +1134,7 @@
         norm2_shift,
     )
 
-    def joined(kind):
-        return jnp.concatenate(
-            [
-                packed[128 * kind : 128 * kind + 128],
-                packed[384 + 64 * kind : 448 + 64 * kind],
-            ]
-        ).astype(F32).T
-
-    def joined_bias(kind):
-        return jnp.concatenate(
-            [
-                bias[0, 128 * kind : 128 * kind + 128],
-                bias[0, 384 + 64 * kind : 448 + 64 * kind],
-            ]
-        )
-
-    return (
-        result,
-        input_grad,
-        joined(0),
-        joined_bias(0),
-        joined(1),
-        joined(2),
-        joined_bias(2),
-        out_sum.astype(F32),
-        sums[0],
-        sums[1],
-        sums[2],
-        in_sum.astype(F32),
-        sums[6],
-        down_sum.astype(F32),
-        sums[3],
-        sums[4],
-        sums[5],
-    )
+    return finish(result, input_grad, in_sum, down_sum, packed, out_sum, sums, bias)
 
 
 def solution(mesh):

time: 213 us -> 199 us (0.934)
  local copies, waits for them, and re-layouts: 8.26 us -> 0 us
  other arithmetic: 6.52 us -> 0 us
    pallas_call x0 -> x1, Pallas kernels: none -> 6.58 us  [finish(): pl.pallas_call(finish_kernel, in_specs=[hbm] * 6 + [vmem] * 2, out_specs=...]
    pallas_call x1, Pallas kernels: 196 us -> 191 us  [layer_call(): pl.pallas_call(layer_kernel, in_specs=[smem] + [hbm] * 8 + [vmem] * (3 +...]
    convert_element_type x3 -> x0, other arithmetic: 4.01 us -> none  [the longest x1 1.58 us: local(): in_sum.astype(F32)]
    slice x3 -> x0, local copies, waits for them, and re-layouts: 3.91 us -> none  [the longest x1 1.75 us: local(): sums[5]]
    unnamed x12 -> x0, local copies, waits for them, and re-layouts: 2.94 us -> none
where the time goes in v3:
time: 199 us; the launch traced here: 198 us
  Pallas kernels  198 us (99%)
    pallas_call x1, Pallas kernels, layer_call(): pl.pallas_call(layer_kernel, in_specs=[smem] + [hbm] * 8 + [vmem] * (3 +...  191 us
    pallas_call x1, Pallas kernels, finish(): pl.pallas_call(finish_kernel, in_specs=[hbm] * 6 + [vmem] * 2, out_specs=...  6.58 us

profile of v3, /device:TPU:0, one launch (start us, length us, event | category | flops | bytes accessed | tf_op | source)
XLA Modules:
  0.0 198.5 jit_solution(8750618951662447476)
XLA Ops:
  0.7 191.0 %layer.1 = (bf16[2,256,768]{2,1,0:T(8,128)(2,1)}, f32[2,256,768]{2,1,0:T(8,128)}, bf16[768,768]{1,0:T(8,128)(2,1)}, bf16[768,768]{1,0:T(8,128)(2,1)}, bf16[576,7...) custom-call(s32[2]{0:T(128)} %quarters.1, ...), custom_call_target="tpu_custom_call" | custom-call | tf_op jit(solution)/shard_map/layer/pallas_call | solution.py:931
  191.7 6.6 %finish.1 = (bf16[2,256,768]{2,1,0:T(8,128)(2,1)}, f32[2,256,768]{2,1,0:T(8,128)}, f32[192,768]{1,0:T(8,128)}, f32[192]{0:T(256)}, f32[192,768]{1,0:T(8,128)}, /...) custom-call(bf16[2,256,768]{2,1,0:T(8,128)(2,1)} %get-tuple-element., ...), custom_call_target="tpu_custom_call" | custom-call | tf_op jit(solution)/shard_map/finish/pallas_call | solution.py:1060

commit v4 on v3

--- a/solution.py
+++ b/solution.py
@@ -232,32 +232,32 @@
 
 
 EVENTS = {
-    "closing": ("d0",),
-    1: ("i1", "d1",),
-    3: ("i3", "d2",),
-    4: ("d0",),
-    "closed": ("s", "d3", "i1", "d1",),
-    7: ("i0", "i3",),
-    8: ("d2",),
-    9: ("s", "i2", "d0", "d3",),
-    10: ("i1",),
-    11: ("i3", "d1",),
-    12: ("s", "i0",),
-    13: ("d2",),
-    14: ("i2",),
-    15: ("s", "d0",),
-    17: ("d3",),
-    "between": ("i1", "d0", "i3", "d1",),
-    18: ("s", "i0", "d2",),
-    20: ("d1", "i2",),
-    21: ("s", "d3",),
-    22: ("d2", "i1",),
-    "start": ("i3", "d3",),
-    "pre": ("i0", "i2",),
-    "tail": ("q0", "o0", "q1", "q0", "o0", "q2", "q1",),
+    0: ("d0",),
+    2: ("i1", "d1",),
+    4: ("i3", "d2",),
+    5: ("d0",),
+    "closed": ("s", "d3",),
+    6: ("i1", "d1",),
+    8: ("i0", "i3",),
+    9: ("s", "d2",),
+    10: ("i2", "d0", "d3",),
+    11: ("i1",),
+    12: ("s", "i3", "d1", "i0",),
+    14: ("d2",),
+    15: ("s", "i2", "d0",),
+    "between": ("d3", "i1", "d0",),
+    "weighed": ("d1", "i3",),
+    18: ("s",),
+    19: ("d2",),
+    20: ("i0",),
+    21: ("s", "d3", "i2", "d1",),
+    23: ("i1",),
+    "start": ("d2", "i3",),
+    "pre": ("d3", "i0",),
+    "tail": ("o0", "q0", "i2", "q1", "q0", "o0", "q2", "q1",),
     "end": (
-        "q0", "i0", "q2", "q1", "i2", "q0", "o0", "q2", "q1", "q0",
-        "q2", "o0", "q1", "q2", "o0",
+        "i0", "q2", "q0", "i2", "q1", "o0", "q0", "q2", "q1", "o0",
+        "q0", "q2", "q1", "o0", "q2",
     ),
 }
 Z_FIRST = ("i1", "i3", "o0",)
@@ -280,7 +280,8 @@
 def layer_body(
     quarters, token_hbm, cot_hbm, in_hbm, down_hbm, low_hbm, out_hbm, lengths, query_bias,
     value_bias, vectors,
-    result, input_grad, in_whole, down_whole, qkv_whole, out_whole, sums_out, bias_out, qkv_hbm,
+    result_hbm, input_hbm, in_out, down_out, qkv_out, out_out, sums_out, bias_out, qkv_hbm,
+    result, input_grad, in_whole, down_whole, qkv_whole, out_whole,
     in_weight, down_weight, context, log_total, segment, low_bias,
     in_term, down_term, qkv_term, out_term, weight_all,
     far, near, cross, sums, hid, gm2, act, slope, gpre, pbuf, grad_low,
@@ -433,7 +434,7 @@
     stride = 2 * batch_bits
     chunks = []
 
-    def chunk(term, first, count, order, give, give_at, take, take_at, whole):
+    def chunk(term, first, count, order, give, give_at, take, take_at, whole, home):
         size = reduce_plan(count, order)[1]
         chunks.append(
             BatchSum(
@@ -443,24 +444,29 @@
                 whole, sems, len(chunks) * stride,
             )
         )
+        chunks[-1].home = pltpu.make_async_copy(
+            whole.at[first : first + count, :],
+            home.at[first : first + count, :],
+            load_sem.at[40 + len(chunks)],
+        )
         return chunks[-1]
 
     small = reduce_plan(192, up)[1]
     named = {}
 
-    def add_chunks(letter, count, term, give, give_at, take, whole):
+    def add_chunks(letter, count, term, give, give_at, take, whole, home):
         for k in range(count):
             name = letter + str(k)
             named[name] = chunk(
                 term, 192 * k, 192, turned if name in Z_FIRST else up,
                 *((slope, small * (4 + k)) if letter == "i" and k < 2 else (give, give_at + small * k)),
-                take, small * k, whole,
+                take, small * k, whole, home,
             )
 
-    add_chunks("d", 4, down_term, slope, 0, down_take, down_whole)
-    add_chunks("i", 4, in_term, hid, small * 2, in_take, in_whole)
-    add_chunks("q", 3, qkv_term, hid, 0, qkv_take, qkv_whole)
-    add_chunks("o", 1, out_term, hid, small * 3, out_take, out_whole)
+    add_chunks("d", 4, down_term, slope, 0, down_take, down_whole, down_out)
+    add_chunks("i", 4, in_term, hid, small * 2, in_take, in_whole, in_out)
+    add_chunks("q", 3, qkv_term, hid, 0, qkv_take, qkv_whole, qkv_out)
+    add_chunks("o", 1, out_term, hid, small * 3, out_take, out_whole, out_out)
     batch_targets = [{"batch": batch_place ^ (1 << bit)} for bit in up]
     shared_sum = VectorSum(
         vec_values, vec_take, batch_targets + [core_id, chip_id], sems, 12 * stride
@@ -495,7 +501,7 @@
         low_bias[0:1, 384 + 128 * kind : 448 + 128 * kind] = row[:, 128:192]
     for kind in range(3):
         gpre[448 + 128 * kind : 512 + 128 * kind, :] = jnp.zeros((64, gpre.shape[1]), BF)
-    def find_segments(micro, carry):
+    def find_segments(micro):
         ends = jnp.broadcast_to(lengths[micro], (8, rows_all))
         lane = lax.broadcasted_iota(jnp.int32, (8, rows_all), 1)
         shift = 1
@@ -505,10 +511,9 @@
         ends_col = column_of(ends[0:1, :].astype(F32))
         places = lax.broadcasted_iota(jnp.int32, (rows_all, rows_all), 1).astype(F32)
         count = jnp.sum(jnp.where(ends_col <= places, 1.0, 0.0), axis=0, keepdims=True)
-        segment[pl.ds(pl.multiple_of(micro * 8, 8), 8), :] = jnp.broadcast_to(count, (8, rows_all))
-        return carry
-
-    lax.fori_loop(0, 2, find_segments, 0)
+        segment[8 * micro : 8 * micro + 8, :] = jnp.broadcast_to(count, (8, rows_all))
+
+    find_segments(0)
     pl.semaphore_wait(barrier, len(partners))
     for handle in low_loads + [micro_loads[0], out_load]:
         handle.wait()
@@ -533,6 +538,7 @@
 
         @pl.when(index == 4)
         def _():
+            find_segments(1)
             micro_loads[1].wait()
 
         @pl.when(turn == 0)
@@ -737,6 +743,8 @@
     def run(point):
         for name, step in planned[point]:
             (shared_sum if name == "s" else named[name]).advance(step)
+            if name != "s" and step == named[name].last():
+                named[name].home.start()
 
     run("open")
     for handle in late_loads:
@@ -744,6 +752,7 @@
     closing(0)
     run("closing")
     qkv, tokens, grads = gm2, act, gpre
+    homes = [load(result.at[m], result_hbm.at[m]) for m in range(2)]
 
     def micro_rows(micro):
         return pl.ds(pl.multiple_of(micro * rows_all, rows_all), rows_all)
@@ -887,6 +896,7 @@
 
     def final_rows(micro):
         input_grad[micro] = input_grad[micro] + scatter_end(pbuf, micro, 3)
+        homes.append(load(input_grad.at[micro], input_hbm.at[micro]))
 
     final_rows(0)
     run("tail")
@@ -898,6 +908,8 @@
         while reached[name] < named[name].last():
             reached[name] += 1
             named[name].advance(reached[name])
+            if reached[name] == named[name].last():
+                named[name].home.start()
     while reached["s"] < batch_bits + 2:
         reached["s"] += 1
         shared_sum.advance(reached["s"])
@@ -911,6 +923,10 @@
         gather_drain(grad_low, micro, 2)
     for owner in chunks + [shared_sum, bias_sum]:
         owner.drain()
+    for owner in chunks:
+        owner.home.wait()
+    for handle in homes:
+        handle.wait()
 
 
 def layer_call(
@@ -931,7 +947,7 @@
     return pl.pallas_call(
         layer_kernel,
         in_specs=[smem] + [hbm] * 8 + [vmem] * (3 + len(vectors)),
-        out_specs=[vmem] * 8 + [hbm],
+        out_specs=[hbm] * 6 + [vmem] * 2 + [hbm],
         out_shape=[
             jax.ShapeDtypeStruct((micro_count, share, width), BF),
             jax.ShapeDtypeStruct((micro_count, share, width), F32),
@@ -944,6 +960,12 @@
             jax.ShapeDtypeStruct((rows, 3 * WIDE), BF),
         ],
         scratch_shapes=[
+            pltpu.VMEM((micro_count, share, width), BF),
+            pltpu.VMEM((micro_count, share, width), F32),
+            pltpu.VMEM((width, units), BF),
+            pltpu.VMEM((units, width), BF),
+            pltpu.VMEM((576, width), BF),
+            pltpu.VMEM((192, width), BF),
             pltpu.VMEM((width, units), BF),
             pltpu.VMEM((units, width), BF),
             pltpu.VMEM((rows, 192), BF),
@@ -985,7 +1007,7 @@
             pltpu.SemaphoreType.DMA((48,)),
             pltpu.SemaphoreType.DMA((batch_sems,)),
             pltpu.SemaphoreType.DMA((batch_sems,)),
-            pltpu.SemaphoreType.DMA((32,)),
+            pltpu.SemaphoreType.DMA((56,)),
         ],
         compiler_params=pltpu.CompilerParams(
             collective_id=1, has_side_effects=True, vmem_limit_bytes=67_043_328

time: 199 us -> 195 us (0.980)
  Pallas kernels: 198 us -> 194 us
    pallas_call x1, Pallas kernels: 191 us -> 187 us  [layer_call(): pl.pallas_call(layer_kernel, in_specs=[smem] + [hbm] * 8 + [vmem] * (3 +...]
where the time goes in v4:
time: 195 us; the launch traced here: 194 us
  Pallas kernels  194 us (99%)
    pallas_call x1, Pallas kernels, layer_call(): pl.pallas_call(layer_kernel, in_specs=[smem] + [hbm] * 8 + [vmem] * (3 +...  187 us
    pallas_call x1, Pallas kernels, finish(): pl.pallas_call(finish_kernel, in_specs=[hbm] * 6 + [vmem] * 2, out_specs=...  6.58 us

profile of v4, /device:TPU:0, one launch (start us, length us, event | category | flops | bytes accessed | tf_op | source)
XLA Modules:
  0.0 194.5 jit_solution(14886713338208699345)
XLA Ops:
  0.7 187.1 %layer.1 = (bf16[2,256,768]{2,1,0:T(8,128)(2,1)}, f32[2,256,768]{2,1,0:T(8,128)}, bf16[768,768]{1,0:T(8,128)(2,1)}, bf16[768,768]{1,0:T(8,128)(2,1)}, bf16[576,7...) custom-call(s32[2]{0:T(128)} %quarters.1, ...), custom_call_target="tpu_custom_call" | custom-call | tf_op jit(solution)/shard_map/layer/pallas_call | solution.py:947
  187.7 6.6 %finish.1 = (bf16[2,256,768]{2,1,0:T(8,128)(2,1)}, f32[2,256,768]{2,1,0:T(8,128)}, f32[192,768]{1,0:T(8,128)}, f32[192]{0:T(256)}, f32[192,768]{1,0:T(8,128)}, /...) custom-call(bf16[2,256,768]{2,1,0:T(8,128)(2,1)} %get-tuple-element., ...), custom_call_target="tpu_custom_call" | custom-call | tf_op jit(solution)/shard_map/finish/pallas_call | solution.py:1082
